TPU v7x, 256 devices: a whole 4x4x8 slice. The times are simulated.
256 devices in a mesh: role: 2 (over x_lo), grp: 64 (over z, y, core), tp: 2 (over x_hi).
Axes of the slice: x: 4 (x_hi: 2, x_lo: 2; x = x_hi * 2 + x_lo), y: 4, z: 8, core: 2. Of those that a mesh axis runs over, the one named last changes fastest.
Arguments:
- q_new: bfloat16 [2048, 4096], P('grp', ('role', 'tp')), may hold values from -9 to 9
- k_new: bfloat16 [2048, 512], P('grp', ('role', 'tp')), may hold values from -6 to 6
- v_new: bfloat16 [2048, 512], P('grp', ('role', 'tp')), may hold values from -6 to 6
- k_cache: bfloat16 [2048, 128, 512], P('grp', None, ('role', 'tp')), may hold values from -9 to 9
- v_cache: bfloat16 [2048, 128, 512], P('grp', None, ('role', 'tp')), may hold values from -6 to 6
- cache_len: int32 [2048], P('grp'), may hold values from 1 to 127
- cycle_start: int32 [2048], P('grp'), may hold values from 0 to 127
- residual: bfloat16 [2048, 2880], P('grp', ('role', 'tp')), may hold values from -6 to 6
- out_proj: bfloat16 [4096, 2880], P(('role', 'tp')), may hold values from -0.09375 to 0.09375
- norm_gain: float32 [2880], replicated, may hold values from 0.25 to 1.75
- router: bfloat16 [2880, 64], P(('role', 'tp')), may hold values from -0.21875 to 0.21875
- route_ids: int32 [2048, 4], P('grp'), may hold values from 0 to 63, all different within a row; in each aligned block of 32 rows (0 to 31, 32 to 63, ...) at most 4 rows name the same one
- w_gate: bfloat16 [64, 2880, 1440], P('grp', None, ('role', 'tp')), may hold values from -0.109375 to 0.109375
- w_up: bfloat16 [64, 2880, 1440], P('grp', None, ('role', 'tp')), may hold values from -0.109375 to 0.109375
- w_down: bfloat16 [64, 1440, 2880], P('grp', ('role', 'tp')), may hold values from -0.15625 to 0.15625
Outputs:
- attended: bfloat16 [2048, 2880], P('grp', ('role', 'tp'))
- expert_mix: bfloat16 [2048, 2880], P('grp', ('role', 'tp'))
Inputs may be any that keep to these rules, and one draw needn't show every extreme that they name: `route_ids`: the 4 experts of a token differ. Among the tokens of one grp index (aligned blocks of 32 tokens) no expert is named more than 4 times, a bound that some block reaches.
All inputs are finite; a program needn't handle non-finite values.
Results may differ from a plain program's by a relative error of at most 0.017.
Values may be sent and summed in bfloat16 or wider, within the bound.
A program may use at most 64 MiB of HBM per device.

v0:
```python
import jax
import jax.numpy as jnp
from jax import lax
from jax.sharding import PartitionSpec as P

HEADS = 64
KV_HEADS = 8
HD = 64


epsilon = 1e-05


def in_order(pieces, dim):
    lengths = list(pieces.shape[1:])
    lengths[dim] *= pieces.shape[0]
    return jnp.moveaxis(pieces, 0, dim).reshape(lengths)


def sent_to_all(x, axis):
    copies = jnp.broadcast_to(x, (lax.axis_size(axis), *x.shape))
    return lax.all_to_all(copies, axis, split_axis=0, concat_axis=0, tiled=True)


def collect(x, axis, dim):
    return in_order(sent_to_all(x, axis), dim)


def cut_along(x, dim, devices):
    before, after = (x.shape[:dim], x.shape[dim + 1 :])
    return jnp.moveaxis(x.reshape(*before, devices, -1, *after), dim, 0)


def summed_on_arrival(x, axis, dim):
    devices = lax.axis_size(axis)
    pieces = lax.all_to_all(cut_along(x, dim, devices), axis, 0, 0, tiled=True)
    return jnp.sum(pieces.astype(jnp.float32), axis=0)


def over_copies(x, axis):
    everything = sent_to_all(x, axis)
    return jnp.sum(everything, axis=0)


def attend(q_new, k_new, v_new, k_cache, v_cache, cache_len, cycle_start):
    tokens = q_new.shape[0]
    window = k_cache.shape[1]
    kv_local = k_new.shape[1] // HD
    grouped = HEADS // KV_HEADS
    queries = q_new.reshape(tokens, kv_local, grouped, HD)
    cached_keys = k_cache.reshape(tokens, window, kv_local, HD)
    cached_values = v_cache.reshape(tokens, window, kv_local, HD)
    own_key = k_new.reshape(tokens, kv_local, HD)
    own_value = v_new.reshape(tokens, kv_local, HD)
    factor = HD ** (-0.5)
    scores = (
        jnp.einsum("tkgd,tskd->tkgs", queries, cached_keys, preferred_element_type=jnp.float32)
        * factor
    )
    own_score = (
        jnp.einsum("tkgd,tkd->tkg", queries, own_key, preferred_element_type=jnp.float32) * factor
    )
    positions = jnp.arange(window, dtype=jnp.int32)
    usable = (positions[None, :] - cycle_start[:, None]) % window < cache_len[:, None]
    usable = usable[:, None, None, :]
    masked = jnp.where(usable, scores, -1e30)
    highest = jnp.maximum(jnp.max(masked, axis=3), own_score)
    lifted = jnp.where(usable, jnp.exp(masked - highest[..., None]), 0.0)
    own_lift = jnp.exp(own_score - highest)
    denominator = jnp.sum(lifted, axis=3) + own_lift
    weights = (lifted / denominator[..., None]).astype(jnp.bfloat16)
    own_weight = (own_lift / denominator).astype(jnp.bfloat16)
    combined = jnp.einsum(
        "tkgs,tskd->tkgd", weights, cached_values, preferred_element_type=jnp.float32
    )
    combined = (
        combined
        + own_weight.astype(jnp.float32)[..., None] * own_value.astype(jnp.float32)[:, :, None, :]
    )
    return combined.reshape(tokens, -1).astype(jnp.bfloat16)


def slot_tables(route_ids, logits, capacity):
    experts_count = logits.shape[1]
    named = route_ids[:, :, None] == jnp.arange(experts_count, dtype=jnp.int32)
    chosen = jnp.sum(jnp.where(named, logits[:, None, :], 0.0), axis=2)
    lifted = jnp.exp(chosen)
    route_weight = lifted / jnp.sum(lifted, axis=1, keepdims=True)
    counts = jnp.sum(named.astype(jnp.int32), axis=1)
    earlier = jnp.cumsum(counts, axis=0) - counts
    ranks = jnp.sum(jnp.where(named, earlier[:, None, :], 0), axis=2)
    placed = named[:, :, :, None] & (
        ranks[:, :, None, None] == jnp.arange(capacity, dtype=jnp.int32)
    )
    select = jnp.sum(placed.astype(jnp.float32), axis=1).reshape(route_ids.shape[0], -1)
    mixing = jnp.sum(jnp.where(placed, route_weight[:, :, None, None], 0.0), axis=1).reshape(
        route_ids.shape[0], -1
    )
    return (select, mixing)


def serve(received, w_gate, w_up, w_down):
    sources = received.shape[0]
    items = received.shape[1]
    received = collect(received, ("role", "tp"), 2)
    inputs = received.reshape(sources * items, received.shape[2])
    gate_lin = jnp.dot(inputs, w_gate[0], preferred_element_type=jnp.float32)
    up_lin = jnp.dot(inputs, w_up[0], preferred_element_type=jnp.float32)
    activated = (gate_lin * jax.nn.sigmoid(1.702 * gate_lin) * (up_lin + 1.0)).astype(jnp.bfloat16)
    partial_out = jnp.dot(activated, w_down[0], preferred_element_type=jnp.float32).reshape(
        sources, items, -1
    )
    rounded = lax.optimization_barrier(partial_out.astype(jnp.bfloat16))
    summed = summed_on_arrival(rounded.astype(jnp.float32).astype(jnp.bfloat16), ("role", "tp"), 2)
    return lax.all_to_all(
        summed.astype(jnp.bfloat16), "grp", split_axis=0, concat_axis=0, tiled=True
    ).astype(summed.dtype)


def local(
    q_new,
    k_new,
    v_new,
    k_cache,
    v_cache,
    cache_len,
    cycle_start,
    residual,
    out_proj,
    norm_gain,
    router,
    route_ids,
    w_gate,
    w_up,
    w_down,
):
    share = lax.axis_index(("role", "tp"))
    quarter = residual.shape[1]
    full_width = quarter * lax.axis_size(("role", "tp"))
    heads_out = attend(q_new, k_new, v_new, k_cache, v_cache, cache_len, cycle_start)
    projected = jnp.dot(heads_out, out_proj, preferred_element_type=jnp.float32)
    attended = residual.astype(jnp.float32) + summed_on_arrival(
        projected.astype(jnp.bfloat16), ("role", "tp"), 1
    )
    squares = over_copies(jnp.sum(attended * attended, axis=1, keepdims=True), ("role", "tp"))
    scale = lax.rsqrt(squares / full_width + epsilon)
    gain_part = lax.dynamic_slice_in_dim(norm_gain, share * quarter, quarter)
    outgoing = (attended * scale * gain_part).astype(jnp.bfloat16)
    logits = over_copies(
        jnp.dot(outgoing, router, preferred_element_type=jnp.float32), ("role", "tp")
    )
    tokens = route_ids.shape[0]
    experts_count = logits.shape[1]
    capacity = max(3, tokens * route_ids.shape[1] // experts_count + 2)
    select, mixing = slot_tables(route_ids, logits, capacity)
    outbound = jnp.einsum(
        "ts,tf->sf", select.astype(jnp.bfloat16), outgoing, preferred_element_type=jnp.float32
    )
    outbound = outbound.astype(jnp.bfloat16).reshape(experts_count, capacity, -1)
    returned = serve(
        lax.all_to_all(outbound, "grp", split_axis=0, concat_axis=0, tiled=True),
        w_gate,
        w_up,
        w_down,
    )
    stacked = returned.reshape(-1, returned.shape[2])
    combined = jnp.dot(mixing, stacked, precision=lax.Precision.HIGHEST)
    return (attended.astype(jnp.bfloat16), combined.astype(jnp.bfloat16))


def solution(mesh):
    placed = (
        P("grp", ("role", "tp")),
        P("grp", ("role", "tp")),
        P("grp", ("role", "tp")),
        P("grp", None, ("role", "tp")),
        P("grp", None, ("role", "tp")),
        P("grp"),
        P("grp"),
        P("grp", ("role", "tp")),
        P(("role", "tp"), None),
        P(),
        P(("role", "tp"), None),
        P("grp", None),
        P("grp", None, ("role", "tp")),
        P("grp", None, ("role", "tp")),
        P("grp", ("role", "tp"), None),
    )
    return jax.shard_map(
        local,
        mesh=mesh,
        in_specs=placed,
        out_specs=(P("grp", ("role", "tp")), P("grp", ("role", "tp"))),
        check_vma=False,
    )
```

profile of v0, /device:TPU:1, one launch (start us, length us, event | category | flops | bytes accessed | tf_op | source)
XLA Modules:
  0.0 169.8 jit_solution(791310978737080568)
XLA Ops:
  2.4 1.0 reshape.135
  4.1 1.6 copy.74
  5.8 1.4 fusion.36
  8.6 1.6 copy.79
  10.2 2.1 %fusion.15 = bf16[32,2,8,64]{3,2,1,0:T(8,128)(2,1)} fusion(bf16[32,128,2,64]{1,3,2,0:T(8,128)(2,1)S(1)} %bitcast.67, f32[32,2,8,128]{3,2,1,0:T(8,128)S(1)} %get-tuple-element.9, f32[32,2,64]{2,1,0:T(2,128)S(1)} %reshape.142, f32[32,2,8]{2,1,0:T(2,128)} %copy.80, f32[32,2,8]{2,1,0:T(2,128)S(1)} %copy.78, f32[32,2,8]{2,1,0:T(2,128)S(1)} %copy.76, ...), kind=kOutput, calls=%fused_computation.15 | convolution fusion | flops 8749056 | bytes 1402880 | tf_op jit(solution)/shard_map/tkgs,tskd->tkgd/dot_general | solution.py:73
  12.3 1.0 convert_element_type.76
  13.4 4.5 %convolution_convert_fusion.1 = bf16[32,2880]{1,0:T(8,128)(2,1)S(1)} fusion(bf16[32,1024]{1,0:T(8,128)(2,1)S(1)} %convert_element_type.76, bf16[1024,2880]{0,1:T(8,128)(2,1)} %param.23), kind=kOutput, calls=%fused_computation.1 | convolution fusion | flops 188835840 | bytes 6148096 | tf_op jit(solution)/shard_map/dot_general | solution.py:141
  18.9 4.8 %all-to-all-start = ((bf16[4,32,720]{2,1,0:T(8,128)(2,1)}), bf16[4,32,720]{2,1,0:T(8,128)(2,1)S(1)}, u32[]{:S(2)}, u32[]{:S(2)}) async-start(bf16[4,32,720]{2,1,0:T(8,128)(2,1)} %bitcast.63), calls=%async_computation | async-start | bytes 393216 | tf_op jit(solution)/shard_map/all_to_all | solution.py:36
  24.2 4.4 %all-to-all-done = bf16[4,32,720]{2,1,0:T(8,128)(2,1)S(1)} async-done(((bf16[4,32,720]{2,1,0:T(8,128)(2,1)}), bf16[4,32,720]{2,1,0:T(8,128)(2,1)S(1)}, u32[]{:S(2)}, u32[]{:S(2)}) %all-to-all-start) | async-done | bytes 184352 | tf_op jit(solution)/shard_map/all_to_all | solution.py:36
  29.4 3.2 %all-to-all-start.1 = ((f32[4,32,1]{1,2,0:T(1,128)}), f32[4,32,1]{1,2,0:T(1,128)S(1)}, u32[]{:S(2)}, u32[]{:S(2)}) async-start(f32[4,32,1]{1,2,0:T(1,128)} %broadcast_in_dim.87), calls=%async_computation.1 | async-start | bytes 4096 | tf_op jit(solution)/shard_map/all_to_all | solution.py:22
  33.4 3.2 %all-to-all-done.1 = f32[4,32,1]{1,2,0:T(1,128)S(1)} async-done(((f32[4,32,1]{1,2,0:T(1,128)}), f32[4,32,1]{1,2,0:T(1,128)S(1)}, u32[]{:S(2)}, u32[]{:S(2)}) %all-to-all-start.1) | async-done | bytes 544 | tf_op jit(solution)/shard_map/all_to_all | solution.py:22
  38.2 3.3 %all-to-all-start.2 = ((f32[4,1,2048]{2,1,0:T(1,128)}), f32[4,1,2048]{2,1,0:T(1,128)S(1)}, u32[]{:S(2)}, u32[]{:S(2)}) async-start(f32[4,1,2048]{2,1,0:T(1,128)} %reshape.149), calls=%async_computation.2 | async-start | bytes 65536 | tf_op jit(solution)/shard_map/all_to_all | solution.py:22
  41.5 4.2 %all-to-all-done.2 = f32[4,1,2048]{2,1,0:T(1,128)S(1)} async-done(((f32[4,1,2048]{2,1,0:T(1,128)}), f32[4,1,2048]{2,1,0:T(1,128)S(1)}, u32[]{:S(2)}, u32[]{:S(2)}) %all-to-all-start.2) | async-done | bytes 32800 | tf_op jit(solution)/shard_map/all_to_all | solution.py:22
  48.1 31.0 %all_to_all.35 = bf16[64,4,720]{2,1,0:T(4,128)(2,1)S(1)} all-to-all(bf16[64,4,720]{2,1,0:T(4,128)(2,1)S(1)} %reshape.140), channel_id=1, replica_groups=mesh['role'=2,'grp'=64,'tp'=2] {'grp'}, dimensions={0} | all-to-all | bytes 737280 | tf_op jit(solution)/shard_map/all_to_all | solution.py:161
  79.6 22.7 %all_to_all.36 = bf16[4,64,4,720]{3,2,1,0:T(4,128)(2,1)S(1)} all-to-all(bf16[4,64,4,720]{3,2,1,0:T(4,128)(2,1)S(1)} %broadcast_in_dim.93), channel_id=1, replica_groups=mesh['role'=2,'grp'=64,'tp'=2] {'role','tp'}, dimensions={0} | all-to-all | bytes 2949120 | tf_op jit(solution)/shard_map/all_to_all | solution.py:22
  102.3 3.2 %copy.84 = bf16[64,4,4,720]{3,2,1,0:T(4,128)(2,1)} copy(bf16[64,4,4,720]{3,1,0,2:T(4,128)(2,1)S(1)} %bitcast.64) | data formatting | bytes 2949120 | tf_op jit(solution)/shard_map/transpose | solution.py:17
  105.4 4.2 %reshape_reshape.3 = bf16[256,2880]{1,0:T(8,128)(2,1)} reshape(bf16[64,4,4,720]{3,2,1,0:T(4,128)(2,1)} %copy.84) | data formatting | bytes 2949120 | tf_op jit(solution)/shard_map/reshape;reshape | solution.py:106
  109.6 3.0 %fusion.3 = f32[256,360]{0,1:T(8,128)S(1)} fusion(bf16[256,2880]{1,0:T(8,128)(2,1)} %reshape_reshape.3, bf16[1,2880,360]{1,2,0:T(8,128)(2,1)} %param.27), kind=kOutput, calls=%fused_computation.5 | convolution fusion | flops 530841600 | bytes 3916800 | tf_op jit(solution)/shard_map/dot_general | solution.py:107
  113.8 2.1 %convolution_convert_fusion = bf16[64,4,2880]{2,0,1:T(8,128)(2,1)} fusion(bf16[1,360,2880]{2,1,0:T(8,128)(2,1)S(1)} %copy-done, bf16[64,4,360]{2,1,0:T(4,128)(2,1)S(1)} %dot_general.40), kind=kOutput, calls=%fused_computation | convolution fusion | flops 531578880 | bytes 3732480 | tf_op jit(solution)/shard_map/dot_general | solution.py:110
  115.9 5.1 %reshape.141 = bf16[64,4,4,720]{3,2,0,1:T(4,128)(2,1)} reshape(bf16[64,4,2880]{2,0,1:T(8,128)(2,1)} %convolution_convert_fusion) | data formatting | bytes 2949120 | tf_op jit(solution)/shard_map/reshape | solution.py:31
  121.0 1.6 copy.98
  122.7 22.6 %all_to_all.37 = bf16[4,64,4,720]{3,1,2,0:T(8,128)(2,1)} all-to-all(bf16[4,64,4,720]{3,1,2,0:T(8,128)(2,1)S(1)} %bitcast.65), channel_id=1, replica_groups=mesh['role'=2,'grp'=64,'tp'=2] {'role','tp'}, dimensions={0} | all-to-all | bytes 2949120 | tf_op jit(solution)/shard_map/all_to_all | solution.py:36
  145.2 1.7 %reduce_sum.122 = bf16[64,4,720]{2,0,1:T(8,128)(2,1)S(1)} reduce(bf16[4,64,4,720]{3,1,2,0:T(8,128)(2,1)} %all_to_all.37, bf16[]{:T(256)} %constant.52.clone.1), dimensions={0}, to_apply=%region_13.14 | reduce | flops 552960 | bytes 1843202 | tf_op jit(solution)/shard_map/reduce_sum | solution.py:37
  147.2 21.6 %all_to_all.38 = bf16[64,4,720]{2,1,0:T(4,128)(2,1)S(1)} all-to-all(bf16[64,4,720]{2,1,0:T(4,128)(2,1)S(1)} %copy.88), channel_id=1, replica_groups=mesh['role'=2,'grp'=64,'tp'=2] {'grp'}, dimensions={0} | all-to-all | bytes 737280 | tf_op jit(solution)/shard_map/all_to_all | solution.py:115
  (67 shorter events, 13.6 us)
Async XLA Ops:
  0.6 113.2 %copy-start = (bf16[1,360,2880]{2,1,0:T(8,128)(2,1)S(1)}, bf16[1,360,2880]{2,1,0:T(8,128)(2,1)}, u32[]{:S(2)}) copy-start(bf16[1,360,2880]{2,1,0:T(8,128)(2,1)} %param.29) | copy-start | bytes 6220804
  0.6 5.1 %copy-start.7 = (s32[32]{0:T(128)S(1)}, s32[32]{0:T(128)}, u32[]{:S(2)}) copy-start(s32[32]{0:T(128)} %param.21) | copy-start | bytes 388
  0.7 5.1 %copy-start.6 = (s32[32]{0:T(128)S(1)}, s32[32]{0:T(128)}, u32[]{:S(2)}) copy-start(s32[32]{0:T(128)} %param.20) | copy-start | bytes 388
  3.4 0.6 copy-start.2
  13.4 10.4 %copy-start.5 = (s32[32,4]{0,1:T(4,128)S(1)}, s32[32,4]{0,1:T(4,128)}, u32[]{:S(2)}) copy-start(s32[32,4]{0,1:T(4,128)} %param.26) | copy-start | bytes 1540
  13.4 15.3 %copy-start.3 = (bf16[32,720]{1,0:T(8,128)(2,1)S(1)}, bf16[32,720]{1,0:T(8,128)(2,1)}, u32[]{:S(2)}) copy-start(bf16[32,720]{1,0:T(8,128)(2,1)} %param.22) | copy-start | bytes 138244
  13.4 24.0 %copy-start.4 = (bf16[720,64]{0,1:T(8,128)(2,1)S(1)}, bf16[720,64]{0,1:T(8,128)(2,1)}, u32[]{:S(2)}) copy-start(bf16[720,64]{0,1:T(8,128)(2,1)} %param.25) | copy-start | bytes 276484
  18.9 9.7 %all-to-all-start = ((bf16[4,32,720]{2,1,0:T(8,128)(2,1)}), bf16[4,32,720]{2,1,0:T(8,128)(2,1)S(1)}, u32[]{:S(2)}, u32[]{:S(2)}) async-start(bf16[4,32,720]{2,1,0:T(8,128)(2,1)} %bitcast.63), calls=%async_computation | async-start | bytes 393216 | tf_op jit(solution)/shard_map/all_to_all | solution.py:36
  29.4 7.2 %all-to-all-start.1 = ((f32[4,32,1]{1,2,0:T(1,128)}), f32[4,32,1]{1,2,0:T(1,128)S(1)}, u32[]{:S(2)}, u32[]{:S(2)}) async-start(f32[4,32,1]{1,2,0:T(1,128)} %broadcast_in_dim.87), calls=%async_computation.1 | async-start | bytes 4096 | tf_op jit(solution)/shard_map/all_to_all | solution.py:22
  38.2 7.4 %all-to-all-start.2 = ((f32[4,1,2048]{2,1,0:T(1,128)}), f32[4,1,2048]{2,1,0:T(1,128)S(1)}, u32[]{:S(2)}, u32[]{:S(2)}) async-start(f32[4,1,2048]{2,1,0:T(1,128)} %reshape.149), calls=%async_computation.2 | async-start | bytes 65536 | tf_op jit(solution)/shard_map/all_to_all | solution.py:22
  109.6 3.0 %copy-start.1 = (bf16[256,2880]{1,0:T(8,128)(2,1)S(1)}, bf16[256,2880]{1,0:T(8,128)(2,1)}, u32[]{:S(2)}) copy-start(bf16[256,2880]{1,0:T(8,128)(2,1)} %reshape_reshape.3) | copy-start | bytes 4423684
  109.6 3.1 %copy-start.8 = (bf16[1,2880,360]{1,2,0:T(8,128)(2,1)S(1)}, bf16[1,2880,360]{1,2,0:T(8,128)(2,1)}, u32[]{:S(2)}) copy-start(bf16[1,2880,360]{1,2,0:T(8,128)(2,1)} %param.28) | copy-start | bytes 6220804
where the time goes:
time: 171 us; the launch traced here: 170 us
  blocking collectives  97.9 us (57%)
  local copies, waits for them, and re-layouts  27.8 us (16%)
  matrix products  15.5 us (9%)
  waiting for transfers between devices  11.8 us (7%)
  starting transfers between devices  11.3 us (7%)
  other arithmetic  4.47 us (3%)
    all_to_all x1, blocking collectives, local(): lax.all_to_all(outbound, 'grp', split_axis=0, concat_axis=0, tiled=True)  31 us
    all_to_all x1, blocking collectives, sent_to_all(): return lax.all_to_all(copies, axis, split_axis=0, concat_axis=0, tiled=True)  22.7 us
    all_to_all x1, blocking collectives, summed_on_arrival(): pieces = lax.all_to_all(cut_along(x, dim, devices), axis, 0, 0, tiled=True)  22.6 us
    all_to_all x1, blocking collectives, serve(): lax.all_to_all(summed.astype(jnp.bfloat16), 'grp', split_axis=0, concat_a...  21.6 us
    reshape x4, local copies, waits for them, and re-layouts, cut_along(): return jnp.moveaxis(x.reshape(*before, devices, -1, *after), dim, 0)  7.72 us
    all_to_all x2, waiting for transfers between devices, sent_to_all(): return lax.all_to_all(copies, axis, split_axis=0, concat_axis=0, tiled=True)  7.4 us
    all_to_all x2, starting transfers between devices, sent_to_all(): return lax.all_to_all(copies, axis, split_axis=0, concat_axis=0, tiled=True)  6.49 us
    all_to_all x1, starting transfers between devices, summed_on_arrival(): pieces = lax.all_to_all(cut_along(x, dim, devices), axis, 0, 0, tiled=True)  4.83 us
  transfers between devices with their start and end apart: 3, of which 3 were waited for; matrix products, arithmetic and copies ran while one was open for 1% of the time, Pallas kernels for 0%

commit v1 on v0

v1 whole, which is shorter than its diff:
```python
import jax
import jax.numpy as jnp
from jax import lax
from jax.experimental import pallas as pl
from jax.experimental.pallas import tpu as pltpu
from jax.sharding import PartitionSpec as P

HEADS = 64
KV_HEADS = 8
HD = 64
EPS = 1e-05
ND = 4
QW = 720
PW = 768
HW = PW // 2
NG = 64
NB = 4
BM = NG // NB
BR = BM * 4
MESH = pl.DeviceIdType.MESH
BF = jnp.bfloat16
F32 = jnp.float32


def attend(q_new, k_new, v_new, k_cache, v_cache, cache_len, cycle_start):
    tokens = q_new.shape[0]
    window = k_cache.shape[1]
    kv_local = k_new.shape[1] // HD
    grouped = HEADS // KV_HEADS
    queries = q_new.reshape(tokens, kv_local, grouped, HD)
    cached_keys = k_cache.reshape(tokens, window, kv_local, HD)
    cached_values = v_cache.reshape(tokens, window, kv_local, HD)
    own_key = k_new.reshape(tokens, kv_local, HD)
    own_value = v_new.reshape(tokens, kv_local, HD)
    factor = HD ** (-0.5)
    scores = (
        jnp.einsum("tkgd,tskd->tkgs", queries, cached_keys, preferred_element_type=jnp.float32)
        * factor
    )
    own_score = (
        jnp.einsum("tkgd,tkd->tkg", queries, own_key, preferred_element_type=jnp.float32) * factor
    )
    positions = jnp.arange(window, dtype=jnp.int32)
    usable = (positions[None, :] - cycle_start[:, None]) % window < cache_len[:, None]
    usable = usable[:, None, None, :]
    masked = jnp.where(usable, scores, -1e30)
    highest = jnp.maximum(jnp.max(masked, axis=3), own_score)
    lifted = jnp.where(usable, jnp.exp(masked - highest[..., None]), 0.0)
    own_lift = jnp.exp(own_score - highest)
    denominator = jnp.sum(lifted, axis=3) + own_lift
    weights = (lifted / denominator[..., None]).astype(jnp.bfloat16)
    own_weight = (own_lift / denominator).astype(jnp.bfloat16)
    combined = jnp.einsum(
        "tkgs,tskd->tkgd", weights, cached_values, preferred_element_type=jnp.float32
    )
    combined = (
        combined
        + own_weight.astype(jnp.float32)[..., None] * own_value.astype(jnp.float32)[:, :, None, :]
    )
    return combined.reshape(tokens, -1).astype(jnp.bfloat16)


def x_of(pos):
    role = pos % 2
    tp = pos // 2
    return {"role": role, "tp": tp}, role * 2 + tp


def grp_shift(z, y, c, k, sign):
    j = k // 8
    half = (j + 1) // 2
    dz = (j % 2) * half + (1 - j % 2) * (8 - half)
    dy = (k // 2) % 4
    dc = k % 2
    if sign < 0:
        dz = 8 - dz
        dy = 4 - dy
    return (((z + dz) % 8) * 4 + (y + dy) % 4) * 2 + (c + dc) % 2


def wait_bytes(ref, sem):
    pltpu.make_async_copy(ref, ref, sem).wait()


def stage(
    proj, resid, gain, router, ids_row, ids_col, wg_hbm, wu_hbm, wd_hbm,
    att_out, mix_out,
    wg, wu, wd, wda, rs, stats, stats_in, send, recv, s1s, s1r, s2s, s2r, own, rsend, rrecv,
    w_sem, rs_ss, rs_rs, st_ss, st_rs, a_ss, a_rs, x_ss, x_rs, f_ss, f_rs,
    p_ss, p_rs, q_ss, q_rs, b_ss, b_rs, l_sem,
):
    r = lax.axis_index("role")
    g = lax.axis_index("grp")
    t = lax.axis_index("tp")
    x = t * 2 + r
    z = g // 8
    y = (g // 2) % 4
    c = g % 2
    me_q = r * 2 + t
    right, right_q = x_of((x + 1) % 4)
    left, left_q = x_of((x + 3) % 4)
    opp, opp_q = x_of((x + 2) % 4)
    peers = (left, right, opp)
    blocks = (me_q, left_q, right_q, opp_q)

    barrier = pltpu.get_barrier_semaphore()
    for peer in peers:
        pl.semaphore_signal(barrier, inc=1, device_id=peer, device_id_type=MESH)

    def greet(k, carry):
        pl.semaphore_signal(
            barrier, inc=1, device_id={"grp": grp_shift(z, y, c, k, 1)}, device_id_type=MESH
        )
        return carry

    lax.fori_loop(1, NG, greet, 0)
    loads = [
        pltpu.make_async_copy(wg_hbm, wg.at[0 : ND * QW], w_sem.at[0]),
        pltpu.make_async_copy(wu_hbm, wu.at[0 : ND * QW], w_sem.at[1]),
        pltpu.make_async_copy(wd_hbm, wd, w_sem.at[2]),
    ]
    for load in loads:
        load.start()
    wg[ND * QW :, :] = jnp.zeros((48, wg.shape[1]), BF)
    wu[ND * QW :, :] = jnp.zeros((48, wu.shape[1]), BF)

    def experts_of(rows):
        return grp_shift(z, y, c, rows // 8, 1), (rows // 4) % 2, rows % 4

    slot = lax.broadcasted_iota(jnp.int32, (NG * 8, 1), 0)
    expert, part, rank = experts_of(slot)
    hit = jnp.zeros((NG * 8, 64), jnp.bool_)
    for k in range(4):
        hit = hit | (ids_row[k : k + 1, :] == expert)
    lane = lax.broadcasted_iota(jnp.int32, (64, 64), 1)
    sub = lax.broadcasted_iota(jnp.int32, (64, 64), 0)
    upper = jnp.where((sub < lane) & (sub // 32 == lane // 32), 1.0, 0.0).astype(BF)
    lower = jnp.where((lane < sub) & (sub // 32 == lane // 32), 1.0, 0.0).astype(BF)
    hit_f = jnp.where(hit, 1.0, 0.0)
    earlier = jnp.dot(hit_f.astype(BF), upper, preferred_element_type=F32)
    side = lax.broadcasted_iota(jnp.int32, (NG * 8, 64), 1) // 32
    pick = jnp.where(
        (earlier == rank.astype(F32)) & (side == part), hit_f, 0.0
    ).astype(BF)

    slot_l = lax.broadcasted_iota(jnp.int32, (1, NG * 8), 1)
    expert_l, part_l, rank_l = experts_of(slot_l)
    hit_l = jnp.zeros((64, NG * 8), jnp.bool_)
    for k in range(4):
        hit_l = hit_l | (ids_col[:, k : k + 1] == expert_l)
    hit_lf = jnp.where(hit_l, 1.0, 0.0)
    earlier_l = jnp.dot(lower, hit_lf.astype(BF), preferred_element_type=F32)
    side_l = lax.broadcasted_iota(jnp.int32, (64, NG * 8), 0) // 32
    pick_l = jnp.where(
        (earlier_l == rank_l.astype(F32)) & (side_l == part_l), hit_lf, 0.0
    )
    to_slot = jnp.where(
        lax.broadcasted_iota(jnp.int32, (64, NG * 8), 0) == expert_l, 1.0, 0.0
    ).astype(BF)

    pl.semaphore_wait(barrier, NG - 1 + 3)

    sums = []
    for i, (peer, block) in enumerate(zip(peers, (left_q, right_q, opp_q))):
        sums.append(
            pltpu.make_async_remote_copy(
                src_ref=proj.at[block], dst_ref=rs.at[i], send_sem=rs_ss.at[i],
                recv_sem=rs_rs.at[i], device_id=peer, device_id_type=MESH,
            )
        )
    for copy in sums:
        copy.start()
    attended = resid[...].astype(F32) + proj[me_q].astype(F32)
    for i, copy in enumerate(sums):
        copy.wait_recv()
        attended = attended + rs[i].astype(F32)
    att = attended.astype(BF)
    halves = jnp.concatenate([att[:, :HW], att[:, HW:]], axis=0)
    send[...] = (
        jnp.dot(pick, halves, preferred_element_type=F32).reshape(NG, 8, HW).astype(BF)
    )
    att_out[...] = att[:, :QW]
    weighted = (attended * gain[pl.ds(me_q, 1), :]).astype(BF)
    stats[...] = jnp.zeros(stats.shape, F32)
    stats[:, 0:64] = jnp.dot(weighted[:, :QW], router[...], preferred_element_type=F32)
    stats[:, 64:65] = jnp.sum(attended * attended, axis=1, keepdims=True)

    own_msg = pltpu.make_async_copy(send.at[0], recv.at[0, 0], a_rs.at[0])
    own_msg.start()

    def post(k, carry):
        pltpu.make_async_remote_copy(
            src_ref=send.at[k], dst_ref=recv.at[0, k], send_sem=a_ss, recv_sem=a_rs.at[k // BM],
            device_id={"grp": grp_shift(z, y, c, k, 1)}, device_id_type=MESH,
        ).start()
        return carry

    lax.fori_loop(1, NG, post, 0)
    shared = [
        pltpu.make_async_remote_copy(
            src_ref=stats, dst_ref=stats_in.at[i], send_sem=st_ss.at[i],
            recv_sem=st_rs.at[i], device_id=peer, device_id_type=MESH,
        )
        for i, peer in enumerate(peers)
    ]
    for copy in shared:
        copy.start()

    loads[2].wait()
    tail = jnp.zeros((4, 360, PW - QW), BF)
    wda[:, :, QW:] = tail

    def shift_rows(i, carry):
        rows = pl.ds(pl.multiple_of(i * 16, 16), 16)
        block = wd[rows, :].astype(F32)
        for q in range(4):
            wda[q, rows, 0:QW] = block[:, QW * q : QW * (q + 1)].astype(BF)
        return carry

    lax.fori_loop(0, 22, shift_rows, 0)
    block = wd[352:360, :].astype(F32)
    for q in range(4):
        wda[q, 352:360, 0:QW] = block[:, QW * q : QW * (q + 1)].astype(BF)
    loads[0].wait()
    loads[1].wait()

    total = stats[...]
    for i, copy in enumerate(shared):
        copy.wait_recv()
        total = total + stats_in[i]
    scale = lax.rsqrt(total[:, 64:65] / (ND * QW) + EPS)
    logits = total[:, 0:64] * scale
    named = jnp.zeros((32, 64), jnp.bool_)
    experts = lax.broadcasted_iota(jnp.int32, (32, 64), 1)
    for k in range(4):
        named = named | (ids_col[0:32, k : k + 1] == experts)
    lifted = jnp.where(named, jnp.exp(jnp.where(named, logits, 0.0)), 0.0)
    weight = lifted / jnp.sum(lifted, axis=1, keepdims=True)
    weight = jnp.concatenate([weight, weight], axis=0)
    w_high = weight.astype(BF)
    w_low = (weight - w_high.astype(F32)).astype(BF)
    mix_high = (jnp.dot(w_high, to_slot, preferred_element_type=F32) * pick_l).astype(BF)
    mix_low = (jnp.dot(w_low, to_slot, preferred_element_type=F32) * pick_l).astype(BF)

    first4 = lax.broadcasted_iota(jnp.int32, (BM // 2, 8, HW), 1) < 4

    def to_side(src, dst, ss, rs_, peer):
        return pltpu.make_async_remote_copy(
            src_ref=src, dst_ref=dst, send_sem=ss, recv_sem=rs_, device_id=peer,
            device_id_type=MESH,
        )

    def span(b):
        return pl.ds(b * BM, BM)

    def ring_out(b):
        wait_bytes(recv.at[0, span(b)], a_rs.at[b])
        copies = (
            to_side(recv.at[0, span(b)], recv.at[1, span(b)], x_ss.at[b, 0], x_rs.at[b, 0], right),
            to_side(recv.at[0, span(b)], recv.at[2, span(b)], x_ss.at[b, 1], x_rs.at[b, 1], left),
        )
        for copy in copies:
            copy.start()
        return copies

    def ring_on(b, copies):
        first, second = pl.ds(b * BM, BM // 2), pl.ds(b * BM + BM // 2, BM // 2)
        copies[0].wait_recv()
        on_right = to_side(
            recv.at[1, first], recv.at[3, first], f_ss.at[b, 0], f_rs.at[b, 0], right
        )
        on_right.start()
        copies[1].wait_recv()
        on_left = to_side(
            recv.at[2, second], recv.at[3, second], f_ss.at[b, 1], f_rs.at[b, 1], left
        )
        on_left.start()
        return on_right, on_left

    def expert_out(b, forwards):
        for copy in forwards:
            copy.wait_recv()
        gate = jnp.zeros((BR, wg.shape[1]), F32)
        up = jnp.zeros((BR, wu.shape[1]), F32)
        square = jnp.zeros((BR, 1), F32)
        for i, q in enumerate(blocks):
            rows = recv[i, span(b)].astype(F32).reshape(BM // 2, 2, 8, HW)
            even, odd = rows[:, 0], rows[:, 1]
            low = jnp.where(first4, even, pltpu.roll(odd, 4, 1)).reshape(BR, HW)
            high = jnp.where(first4, pltpu.roll(even, 4, 1), odd).reshape(BR, HW)
            feats = jnp.concatenate([low, high], axis=1)
            square = square + jnp.sum(feats * feats, axis=1, keepdims=True)
            feats = (feats * gain[pl.ds(q, 1), :]).astype(BF)
            depth = pl.ds(pl.multiple_of(q * QW, 16), PW)
            gate = gate + jnp.dot(feats, wg[depth, :], preferred_element_type=F32)
            up = up + jnp.dot(feats, wu[depth, :], preferred_element_type=F32)
        rms = lax.rsqrt(square / (ND * QW) + EPS)
        gate = gate * rms
        up = up * rms
        act = (gate * jax.nn.sigmoid(1.702 * gate) * (up + 1.0)).astype(BF)
        out = jnp.dot(act, wda[opp_q], preferred_element_type=F32).astype(BF)
        s1s[b, 0] = out[: BR // 2]
        s1s[b, 1] = out[BR // 2 :]
        copies = (
            to_side(s1s.at[b, 0], s1r.at[b, 0], p_ss.at[b, 0], p_rs.at[b, 0], right),
            to_side(s1s.at[b, 1], s1r.at[b, 1], p_ss.at[b, 1], p_rs.at[b, 1], left),
        )
        for copy in copies:
            copy.start()
        for i, q in enumerate((me_q, right_q, left_q)):
            out = jnp.dot(act, wda[q], preferred_element_type=F32)
            own[b, i] = out.astype(BF).astype(F32)
        return copies

    def sum_on(b, firsts):
        firsts[0].wait_recv()
        to_right = own[b, 1]
        s2s[b, 0, 0 : BR // 2] = (to_right[: BR // 2] + s1r[b, 0].astype(F32)).astype(BF)
        s2s[b, 0, BR // 2 :] = to_right[BR // 2 :].astype(BF)
        firsts[1].wait_recv()
        to_left = own[b, 2]
        s2s[b, 1, 0 : BR // 2] = to_left[: BR // 2].astype(BF)
        s2s[b, 1, BR // 2 :] = (to_left[BR // 2 :] + s1r[b, 1].astype(F32)).astype(BF)
        copies = (
            to_side(s2s.at[b, 0], s2r.at[b, 0], q_ss.at[b, 0], q_rs.at[b, 0], right),
            to_side(s2s.at[b, 1], s2r.at[b, 1], q_ss.at[b, 1], q_rs.at[b, 1], left),
        )
        for copy in copies:
            copy.start()
        return copies

    def give_back(b, seconds):
        for copy in seconds:
            copy.wait_recv()
        rows = own[b, 0] + s2r[b, 0].astype(F32) + s2r[b, 1].astype(F32)
        low = rows[:, :HW].reshape(BM // 2, 8, HW)
        high = rows[:, HW:].reshape(BM // 2, 8, HW)
        even = jnp.where(first4, low, pltpu.roll(high, 4, 1))
        odd = jnp.where(first4, pltpu.roll(low, 4, 1), high)
        rsend[b * BM : (b + 1) * BM] = (
            jnp.stack([even, odd], axis=1).reshape(BM, 8, HW).astype(BF)
        )
        if b == 0:
            pltpu.make_async_copy(rsend.at[0], rrecv.at[0], b_rs.at[0]).start()

        def post_back(k, carry):
            pltpu.make_async_remote_copy(
                src_ref=rsend.at[k], dst_ref=rrecv.at[k], send_sem=b_ss, recv_sem=b_rs.at[b],
                device_id={"grp": grp_shift(z, y, c, k, -1)}, device_id_type=MESH,
            ).start()
            return carry

        lax.fori_loop(max(1, b * BM), (b + 1) * BM, post_back, 0)

    out_c = [None] * NB
    on_c = [None] * NB
    one_c = [None] * NB
    two_c = [None] * NB
    out_c[0] = ring_out(0)
    out_c[1] = ring_out(1)
    on_c[0] = ring_on(0, out_c[0])
    out_c[2] = ring_out(2)
    on_c[1] = ring_on(1, out_c[1])
    out_c[3] = ring_out(3)
    one_c[0] = expert_out(0, on_c[0])
    on_c[2] = ring_on(2, out_c[2])
    one_c[1] = expert_out(1, on_c[1])
    on_c[3] = ring_on(3, out_c[3])
    two_c[0] = sum_on(0, one_c[0])
    one_c[2] = expert_out(2, on_c[2])
    two_c[1] = sum_on(1, one_c[1])
    give_back(0, two_c[0])
    one_c[3] = expert_out(3, on_c[3])
    two_c[2] = sum_on(2, one_c[2])
    give_back(1, two_c[1])
    two_c[3] = sum_on(3, one_c[3])
    give_back(2, two_c[2])
    give_back(3, two_c[3])

    mixed = jnp.zeros((64, HW), F32)
    for b in range(NB):
        wait_bytes(rrecv.at[span(b)], b_rs.at[b])
        rows = rrecv[b * BM : (b + 1) * BM].reshape(BM * 8, HW)
        cols = slice(b * BM * 8, (b + 1) * BM * 8)
        mixed = mixed + jnp.dot(mix_high[:, cols], rows, preferred_element_type=F32)
        mixed = mixed + jnp.dot(mix_low[:, cols], rows, preferred_element_type=F32)
    mixed = mixed.astype(BF)
    mix_out[:, 0:HW] = mixed[0:32]
    mix_out[:, HW:QW] = mixed[32:64, 0 : QW - HW]

    for copy in sums + shared:
        copy.wait_send()
    wait_bytes(send.at[pl.ds(1, NG - 1)], a_ss)
    wait_bytes(rsend.at[pl.ds(1, NG - 1)], b_ss)
    for group in (out_c, on_c, one_c, two_c):
        for pair in group:
            for copy in pair:
                copy.wait_send()


def local(
    q_new, k_new, v_new, k_cache, v_cache, cache_len, cycle_start, residual, out_proj,
    norm_gain, router, route_ids, w_gate, w_up, w_down,
):
    heads_out = attend(q_new, k_new, v_new, k_cache, v_cache, cache_len, cycle_start)
    projected = jnp.dot(heads_out, out_proj, preferred_element_type=F32).astype(BF)
    spare = PW - QW
    proj = jnp.pad(
        jnp.moveaxis(projected.reshape(-1, ND, QW), 1, 0), ((0, 0), (0, 0), (0, spare))
    )
    resid = jnp.pad(residual, ((0, 0), (0, spare)))
    gain = jnp.pad(norm_gain.reshape(ND, QW), ((0, 0), (0, spare)))
    ids_col = jnp.concatenate([route_ids, route_ids], axis=0)
    ids_row = ids_col.T
    vmem = pl.BlockSpec(memory_space=pltpu.VMEM)
    hbm = pl.BlockSpec(memory_space=pl.ANY)
    dma = pltpu.SemaphoreType.DMA
    half_ff = w_gate.shape[2]
    return pl.pallas_call(
        stage,
        out_shape=(
            jax.ShapeDtypeStruct(residual.shape, BF),
            jax.ShapeDtypeStruct(residual.shape, BF),
        ),
        in_specs=[vmem] * 6 + [hbm] * 3,
        out_specs=(vmem, vmem),
        scratch_shapes=[
            pltpu.VMEM((ND * QW + 48, half_ff), BF),
            pltpu.VMEM((ND * QW + 48, half_ff), BF),
            pltpu.VMEM((half_ff, ND * QW), BF),
            pltpu.VMEM((ND, half_ff, PW), BF),
            pltpu.VMEM((3, 32, PW), BF),
            pltpu.VMEM((32, 128), F32),
            pltpu.VMEM((3, 32, 128), F32),
            pltpu.VMEM((NG, 8, HW), BF),
            pltpu.VMEM((ND, NG, 8, HW), BF),
            pltpu.VMEM((NB, 2, BR // 2, PW), BF),
            pltpu.VMEM((NB, 2, BR // 2, PW), BF),
            pltpu.VMEM((NB, 2, BR, PW), BF),
            pltpu.VMEM((NB, 2, BR, PW), BF),
            pltpu.VMEM((NB, 3, BR, PW), F32),
            pltpu.VMEM((NG, 8, HW), BF),
            pltpu.VMEM((NG, 8, HW), BF),
            dma((3,)),
            dma((3,)),
            dma((3,)),
            dma((3,)),
            dma((3,)),
            dma,
            dma((NB,)),
            dma((NB, 2)),
            dma((NB, 2)),
            dma((NB, 2)),
            dma((NB, 2)),
            dma((NB, 2)),
            dma((NB, 2)),
            dma((NB, 2)),
            dma((NB, 2)),
            dma,
            dma((NB,)),
            dma,
        ],
        compiler_params=pltpu.CompilerParams(collective_id=0, has_side_effects=True),
        name="experts",
    )(proj, resid, gain, router, ids_row, ids_col, w_gate[0], w_up[0], w_down[0])


def solution(mesh):
    placed = (
        P("grp", ("role", "tp")),
        P("grp", ("role", "tp")),
        P("grp", ("role", "tp")),
        P("grp", None, ("role", "tp")),
        P("grp", None, ("role", "tp")),
        P("grp"),
        P("grp"),
        P("grp", ("role", "tp")),
        P(("role", "tp"), None),
        P(),
        P(("role", "tp"), None),
        P("grp", None),
        P("grp", None, ("role", "tp")),
        P("grp", None, ("role", "tp")),
        P("grp", ("role", "tp"), None),
    )
    return jax.shard_map(
        local,
        mesh=mesh,
        in_specs=placed,
        out_specs=(P("grp", ("role", "tp")), P("grp", ("role", "tp"))),
        check_vma=False,
    )
```

time: 171 us -> 97.9 us (0.57)
  blocking collectives: 97.9 us -> 0 us
  Pallas kernels: 0 us -> 66.6 us
  waiting for transfers between devices: 11.8 us -> 0 us
  starting transfers between devices: 11.3 us -> 0 us
  matrix products: 15.5 us -> 6.07 us
  local copies, waits for them, and re-layouts: 27.8 us -> 21.4 us
  other arithmetic: 4.47 us -> 2.43 us
    all_to_all x4 -> x0, blocking collectives: 97.9 us -> none  [the longest x1 31 us: local(): lax.all_to_all(outbound, 'grp', split_axis=0, concat_axis=0, tiled=True)]
    pallas_call x0 -> x1, Pallas kernels: none -> 66.6 us  [local(): pl.pallas_call(stage, out_shape=(jax.ShapeDtypeStruct(residual.shape, BF)...]
    all_to_all x3 -> x0, waiting for transfers between devices: 11.8 us -> none  [the longest x2 7.4 us: sent_to_all(): return lax.all_to_all(copies, axis, split_axis=0, concat_axis=0, tiled=True)]
    all_to_all x3 -> x0, starting transfers between devices: 11.3 us -> none  [the longest x2 6.49 us: sent_to_all(): return lax.all_to_all(copies, axis, split_axis=0, concat_axis=0, tiled=True)]
    unnamed x22 -> x11, local copies, waits for them, and re-layouts: 4.68 us -> 13.7 us
    dot_general x7 -> x1, matrix products: 11.8 us -> 4.66 us  [local(): jnp.dot(heads_out, out_proj, preferred_element_type=F32).astype(BF)]
    reshape x5 -> x3, local copies, waits for them, and re-layouts: 7.83 us -> 1.1 us  [the longest x1 0.78 us: local(): gain = jnp.pad(norm_gain.reshape(ND, QW), ((0, 0), (0, spare)))]
    another operation x1 -> x0, local copies, waits for them, and re-layouts: 4.21 us -> none  [serve(): inputs = received.reshape(sources * items, received.shape[2])]
  transfers between devices with their start and end apart: 3 -> 0, of which waited for: 3 -> 0; matrix products, arithmetic and copies ran while one was open for 1% -> 0% of each run, Pallas kernels for 0% -> 0%
where the time goes in v1:
time: 97.9 us; the launch traced here: 97.3 us
  Pallas kernels  66.6 us (68%)
  local copies, waits for them, and re-layouts  21.4 us (22%)
  matrix products  6.07 us (6%)
  other arithmetic  2.43 us (2%)
    pallas_call x1, Pallas kernels, local(): pl.pallas_call(stage, out_shape=(jax.ShapeDtypeStruct(residual.shape, BF)...  66.6 us
    unnamed x11, local copies, waits for them, and re-layouts  13.7 us
    dot_general x1, matrix products, local(): jnp.dot(heads_out, out_proj, preferred_element_type=F32).astype(BF)  4.66 us

profile of v1, /device:TPU:1, one launch (start us, length us, event | category | flops | bytes accessed | tf_op | source)
XLA Modules:
  0.0 97.3 jit_solution(2040098101658717066)
XLA Ops:
  0.6 0.8 fusion.8
  1.4 1.4 %pad_add_fusion = (s32[64,4]{0,1:T(4,128)S(1)}, s32[4,64]{1,0:T(4,128)}) fusion(s32[32,4]{0,1:T(4,128)} %param.26), kind=kLoop, calls=%fused_computation.27 | loop fusion | flops 256 | bytes 2560 | tf_op jit(solution)/shard_map/concatenate | solution.py:413
  2.8 0.8 reshape.80
  3.5 0.6 pad.14.gain
  4.2 0.7 copy.62.ids_col
  4.9 0.8 reshape.85
  5.6 0.8 reshape.81
  6.4 1.4 %pad.13.resid = bf16[32,768]{1,0:T(8,128)(2,1)} pad(bf16[32,720]{1,0:T(8,128)(2,1)} %param.22, bf16[]{:T(256)} %constant.27.clone.1), padding=0_0x0_48 | pad | bytes 95234 | tf_op jit(solution)/shard_map/jit(_pad)/pad | solution.py:411
  7.9 1.0 %reshape.75 = bf16[32,2,8,64]{3,2,1,0:T(8,128)(2,1)S(1)} reshape(bf16[32,1024]{1,0:T(8,128)(2,1)} %param.15) | data formatting | bytes 131072 | tf_op jit(solution)/shard_map/reshape | solution.py:30
  8.9 0.2 fusion.18
  9.1 1.8 %copy.61.router = bf16[720,64]{1,0:T(8,128)(2,1)} copy(bf16[720,64]{0,1:T(8,128)(2,1)} %param.25) | data formatting | bytes 184320 | tf_op args[10]
  11.0 1.6 %copy.51 = bf16[32,128,128]{1,2,0:T(8,128)(2,1)S(1)} copy(bf16[32,128,128]{2,1,0:T(8,128)(2,1)} %param.18) | data formatting | bytes 2097152 | tf_op args[3]
  12.6 0.5 fusion.17
  13.2 0.3 fusion.2
  13.8 0.7 copy.56
  14.5 0.7 fusion.1
  15.4 4.7 %convolution_convert_fusion = bf16[32,2880]{1,0:T(8,128)(2,1)S(1)} fusion(bf16[32,1024]{1,0:T(8,128)(2,1)S(1)} %convert_element_type.40, bf16[1024,2880]{0,1:T(8,128)(2,1)} %param.23), kind=kOutput, calls=%fused_computation | convolution fusion | flops 188835840 | bytes 6148096 | tf_op jit(solution)/shard_map/dot_general | solution.py:406
  20.0 0.3 reshape.79
  20.4 0.7 pad.12.proj
  21.1 2.6 %copy.59 = bf16[1,2880,360]{2,1,0:T(8,128)(2,1)} copy(bf16[1,2880,360]{1,2,0:T(8,128)(2,1)S(1)} %copy-done) | data formatting | bytes 4147200 | tf_op args[12]
  23.7 4.1 %copy.60 = bf16[1,2880,360]{2,1,0:T(8,128)(2,1)} copy(bf16[1,2880,360]{1,2,0:T(8,128)(2,1)} %param.28) | data formatting | bytes 4147200 | tf_op args[13]
  27.8 66.6 %experts.1 = (bf16[32,720]{1,0:T(8,128)(2,1)}, bf16[32,720]{1,0:T(8,128)(2,1)}) custom-call(bf16[4,32,768]{2,1,0:T(8,128)(2,1)} %pad.12.proj, bf16[32,768]{1,0:T(8,128)(2,1)} %pad.13.resid, f32[4,768]{1,0:T(4,128)} %pad.14.gain, bf16[720,64]{1,0:T(8,128)(2,1)} %copy.61.router, s32[4,64]{1,0:T(4,128)} %get-tuple-element.5.ids_row, s32[64,4]{1,0:T(8,128)} %copy.62.ids_col, ...), custom_call_target="tpu_custom_call" | custom-call | tf_op jit(solution)/shard_map/experts/pallas_call | solution.py:419
  94.4 1.4 %copy.69 = bf16[32,720]{1,0:T(8,128)(2,1)} copy(bf16[32,720]{1,0:T(8,128)(2,1)} %get-tuple-element.10) | data formatting | bytes 92160
  95.8 1.4 %copy.70 = bf16[32,720]{1,0:T(8,128)(2,1)} copy(bf16[32,720]{1,0:T(8,128)(2,1)} %get-tuple-element.11) | data formatting | bytes 92160
  (14 shorter events, 0.7 us)
Async XLA Ops:
  9.1 4.7 %copy-start.1 = (bf16[32,128,128]{2,1,0:T(8,128)(2,1)S(1)}, bf16[32,128,128]{2,1,0:T(8,128)(2,1)}, u32[]{:S(2)}) copy-start(bf16[32,128,128]{2,1,0:T(8,128)(2,1)} %param.19) | copy-start | bytes 3145732
  15.4 5.7 %copy-start = (bf16[1,2880,360]{1,2,0:T(8,128)(2,1)S(1)}, bf16[1,2880,360]{1,2,0:T(8,128)(2,1)}, u32[]{:S(2)}) copy-start(bf16[1,2880,360]{1,2,0:T(8,128)(2,1)} %param.27) | copy-start | bytes 6220804

commit v2 on v1

--- a/solution.py
+++ b/solution.py
@@ -5,8 +5,6 @@
 from jax.experimental.pallas import tpu as pltpu
 from jax.sharding import PartitionSpec as P
 
-HEADS = 64
-KV_HEADS = 8
 HD = 64
 EPS = 1e-05
 ND = 4
@@ -22,42 +20,55 @@
 F32 = jnp.float32
 
 
-def attend(q_new, k_new, v_new, k_cache, v_cache, cache_len, cycle_start):
-    tokens = q_new.shape[0]
-    window = k_cache.shape[1]
-    kv_local = k_new.shape[1] // HD
-    grouped = HEADS // KV_HEADS
-    queries = q_new.reshape(tokens, kv_local, grouped, HD)
-    cached_keys = k_cache.reshape(tokens, window, kv_local, HD)
-    cached_values = v_cache.reshape(tokens, window, kv_local, HD)
-    own_key = k_new.reshape(tokens, kv_local, HD)
-    own_value = v_new.reshape(tokens, kv_local, HD)
-    factor = HD ** (-0.5)
-    scores = (
-        jnp.einsum("tkgd,tskd->tkgs", queries, cached_keys, preferred_element_type=jnp.float32)
-        * factor
-    )
-    own_score = (
-        jnp.einsum("tkgd,tkd->tkg", queries, own_key, preferred_element_type=jnp.float32) * factor
-    )
-    positions = jnp.arange(window, dtype=jnp.int32)
-    usable = (positions[None, :] - cycle_start[:, None]) % window < cache_len[:, None]
-    usable = usable[:, None, None, :]
-    masked = jnp.where(usable, scores, -1e30)
-    highest = jnp.maximum(jnp.max(masked, axis=3), own_score)
-    lifted = jnp.where(usable, jnp.exp(masked - highest[..., None]), 0.0)
-    own_lift = jnp.exp(own_score - highest)
-    denominator = jnp.sum(lifted, axis=3) + own_lift
-    weights = (lifted / denominator[..., None]).astype(jnp.bfloat16)
-    own_weight = (own_lift / denominator).astype(jnp.bfloat16)
-    combined = jnp.einsum(
-        "tkgs,tskd->tkgd", weights, cached_values, preferred_element_type=jnp.float32
-    )
-    combined = (
-        combined
-        + own_weight.astype(jnp.float32)[..., None] * own_value.astype(jnp.float32)[:, :, None, :]
-    )
-    return combined.reshape(tokens, -1).astype(jnp.bfloat16)
+def attend(q_ref, k_new, v_new, keys, values, lens, starts, qs, hs):
+    tokens, window = keys.shape[0], keys.shape[1]
+    sub = lax.broadcasted_iota(jnp.int32, (tokens, tokens), 0)
+    lane = lax.broadcasted_iota(jnp.int32, (tokens, tokens), 1)
+
+    def column(row):
+        return jnp.sum(jnp.where(sub == lane, row.astype(F32), 0.0), axis=1, keepdims=True)
+
+    slot = lax.broadcasted_iota(jnp.int32, (tokens, window), 1).astype(F32)
+    age = slot - column(starts[...])
+    age = jnp.where(age < 0.0, age + window, age)
+    live_all = jnp.where(age < column(lens[...]), 1.0, 0.0)
+    queries = q_ref[...].astype(F32) * HD ** (-0.5)
+    for j in range(8):
+        qs[:, j, :] = queries[:, 128 * j : 128 * (j + 1)]
+    step = 8
+    shape = (step, 8, 128)
+    mine = (lax.broadcasted_iota(jnp.int32, shape, 1) < 4) == (
+        lax.broadcasted_iota(jnp.int32, shape, 2) < HD
+    )
+    key_own = k_new[...].astype(F32)
+    value_own = v_new[...].astype(F32)
+    for start in range(0, tokens, step):
+        rows = slice(start, start + step)
+        pair = qs[rows]
+        heads = jnp.concatenate(
+            [jnp.where(mine, pair, 0.0), jnp.where(mine, pltpu.roll(pair, HD, 2), 0.0)], axis=1
+        )
+        own = jnp.sum(heads * key_own[rows][:, None, :], axis=2, keepdims=True)
+        scores = lax.dot_general(
+            heads.astype(BF), keys[rows], (((2,), (2,)), ((0,), (0,))),
+            preferred_element_type=F32,
+        )
+        live = jnp.broadcast_to(live_all[rows][:, None, :], scores.shape) > 0.5
+        scores = jnp.where(live, scores, -1e30)
+        highest = jnp.maximum(jnp.max(scores, axis=2, keepdims=True), own)
+        lifted = jnp.where(live, jnp.exp(scores - highest), 0.0)
+        own_lift = jnp.exp(own - highest)
+        total = jnp.sum(lifted, axis=2, keepdims=True) + own_lift
+        weights = (lifted / total).astype(BF)
+        own_weight = (own_lift / total).astype(BF).astype(F32)
+        out = lax.dot_general(
+            weights, values[rows], (((2,), (1,)), ((0,), (0,))), preferred_element_type=F32
+        )
+        out = out + own_weight * value_own[rows][:, None, :]
+        hs[rows] = jnp.where(mine, out[:, 0:8], 0.0) + pltpu.roll(
+            jnp.where(mine, out[:, 8:16], 0.0), HD, 2
+        )
+    return jnp.concatenate([hs[:, j, :] for j in range(8)], axis=1).astype(BF)
 
 
 def x_of(pos):
@@ -83,11 +94,14 @@
 
 
 def stage(
-    proj, resid, gain, router, ids_row, ids_col, wg_hbm, wu_hbm, wd_hbm,
+    q_ref, k_new, v_new, k_hbm, v_hbm, lens, starts, resid, wo_hbm, gain_row, router, ids,
+    wg_hbm, wu_hbm, wd_hbm,
     att_out, mix_out,
-    wg, wu, wd, wda, rs, stats, stats_in, send, recv, s1s, s1r, s2s, s2r, own, rsend, rrecv,
+    keys, values, qs, hs, wo, proj, gain,
+    wg, wu, wd, wga, wua, wda, rs, stats, stats_in, send, recv, s1s, s1r, s2s, s2r, own, rsend,
+    rrecv,
     w_sem, rs_ss, rs_rs, st_ss, st_rs, a_ss, a_rs, x_ss, x_rs, f_ss, f_rs,
-    p_ss, p_rs, q_ss, q_rs, b_ss, b_rs, l_sem,
+    p_ss, p_rs, q_ss, q_rs, b_ss, b_rs,
 ):
     r = lax.axis_index("role")
     g = lax.axis_index("grp")
@@ -100,7 +114,7 @@
     right, right_q = x_of((x + 1) % 4)
     left, left_q = x_of((x + 3) % 4)
     opp, opp_q = x_of((x + 2) % 4)
-    peers = (left, right, opp)
+    peers = (opp, left, right)
     blocks = (me_q, left_q, right_q, opp_q)
 
     barrier = pltpu.get_barrier_semaphore()
@@ -115,28 +129,47 @@
 
     lax.fori_loop(1, NG, greet, 0)
     loads = [
-        pltpu.make_async_copy(wg_hbm, wg.at[0 : ND * QW], w_sem.at[0]),
-        pltpu.make_async_copy(wu_hbm, wu.at[0 : ND * QW], w_sem.at[1]),
-        pltpu.make_async_copy(wd_hbm, wd, w_sem.at[2]),
+        pltpu.make_async_copy(src, dst, w_sem.at[i])
+        for i, (src, dst) in enumerate(
+            (
+                (k_hbm, keys), (v_hbm, values), (wo_hbm, wo), (wg_hbm, wg), (wu_hbm, wu),
+                (wd_hbm, wd),
+            )
+        )
     ]
     for load in loads:
         load.start()
-    wg[ND * QW :, :] = jnp.zeros((48, wg.shape[1]), BF)
-    wu[ND * QW :, :] = jnp.zeros((48, wu.shape[1]), BF)
+    gain[...] = jnp.zeros(gain.shape, F32)
+    for q in range(4):
+        gain[q : q + 1, 0:QW] = gain_row[:, QW * q : QW * (q + 1)]
+        proj[q, :, QW:] = jnp.zeros((32, PW - QW), BF)
 
     def experts_of(rows):
         return grp_shift(z, y, c, rows // 8, 1), (rows // 4) % 2, rows % 4
 
     slot = lax.broadcasted_iota(jnp.int32, (NG * 8, 1), 0)
     expert, part, rank = experts_of(slot)
-    hit = jnp.zeros((NG * 8, 64), jnp.bool_)
+    lane = lax.broadcasted_iota(jnp.int32, (64, 32), 1)
+    sub = lax.broadcasted_iota(jnp.int32, (64, 32), 0)
+    ids_f = ids[...].astype(F32)
+    ids_col = [
+        jnp.sum(jnp.where(sub % 32 == lane, ids_f[k : k + 1, :], 0.0), axis=1, keepdims=True)
+        for k in range(4)
+    ]
+    lane = lax.broadcasted_iota(jnp.int32, (32, 64), 1)
+    sub = lax.broadcasted_iota(jnp.int32, (32, 64), 0)
+    ids_row = [
+        jnp.sum(jnp.where(lane % 32 == sub, ids_col[k][0:32], 0.0), axis=0, keepdims=True)
+        for k in range(4)
+    ]
+    expert_f = expert.astype(F32)
+    hit_f = jnp.zeros((NG * 8, 64), F32)
     for k in range(4):
-        hit = hit | (ids_row[k : k + 1, :] == expert)
+        hit_f = jnp.where(ids_row[k] == expert_f, 1.0, hit_f)
     lane = lax.broadcasted_iota(jnp.int32, (64, 64), 1)
     sub = lax.broadcasted_iota(jnp.int32, (64, 64), 0)
     upper = jnp.where((sub < lane) & (sub // 32 == lane // 32), 1.0, 0.0).astype(BF)
     lower = jnp.where((lane < sub) & (sub // 32 == lane // 32), 1.0, 0.0).astype(BF)
-    hit_f = jnp.where(hit, 1.0, 0.0)
     earlier = jnp.dot(hit_f.astype(BF), upper, preferred_element_type=F32)
     side = lax.broadcasted_iota(jnp.int32, (NG * 8, 64), 1) // 32
     pick = jnp.where(
@@ -145,10 +178,10 @@
 
     slot_l = lax.broadcasted_iota(jnp.int32, (1, NG * 8), 1)
     expert_l, part_l, rank_l = experts_of(slot_l)
-    hit_l = jnp.zeros((64, NG * 8), jnp.bool_)
+    expert_lf = expert_l.astype(F32)
+    hit_lf = jnp.zeros((64, NG * 8), F32)
     for k in range(4):
-        hit_l = hit_l | (ids_col[:, k : k + 1] == expert_l)
-    hit_lf = jnp.where(hit_l, 1.0, 0.0)
+        hit_lf = jnp.where(ids_col[k] == expert_lf, 1.0, hit_lf)
     earlier_l = jnp.dot(lower, hit_lf.astype(BF), preferred_element_type=F32)
     side_l = lax.broadcasted_iota(jnp.int32, (64, NG * 8), 0) // 32
     pick_l = jnp.where(
@@ -158,22 +191,31 @@
         lax.broadcasted_iota(jnp.int32, (64, NG * 8), 0) == expert_l, 1.0, 0.0
     ).astype(BF)
 
+    loads[0].wait()
+    loads[1].wait()
+    heads_out = attend(q_ref, k_new, v_new, keys, values, lens, starts, qs, hs)
+    loads[2].wait()
     pl.semaphore_wait(barrier, NG - 1 + 3)
 
     sums = []
-    for i, (peer, block) in enumerate(zip(peers, (left_q, right_q, opp_q))):
-        sums.append(
-            pltpu.make_async_remote_copy(
-                src_ref=proj.at[block], dst_ref=rs.at[i], send_sem=rs_ss.at[i],
-                recv_sem=rs_rs.at[i], device_id=peer, device_id_type=MESH,
+    for i, block in enumerate((opp_q, left_q, right_q, me_q)):
+        rows = pl.ds(pl.multiple_of(block * QW, 16), QW)
+        part_sum = lax.dot_general(
+            heads_out, wo[rows, :], (((1,), (1,)), ((), ())), preferred_element_type=F32
+        )
+        proj[i, :, 0:QW] = part_sum.astype(BF)
+        if i < 3:
+            copy = pltpu.make_async_remote_copy(
+                src_ref=proj.at[i], dst_ref=rs.at[i], send_sem=rs_ss.at[i],
+                recv_sem=rs_rs.at[i], device_id=peers[i], device_id_type=MESH,
             )
-        )
-    for copy in sums:
-        copy.start()
-    attended = resid[...].astype(F32) + proj[me_q].astype(F32)
-    for i, copy in enumerate(sums):
-        copy.wait_recv()
-        attended = attended + rs[i].astype(F32)
+            copy.start()
+            sums.append(copy)
+    attended = proj[3, :, 0:QW].astype(F32) + resid[...].astype(F32)
+    for i in (1, 2, 0):
+        sums[i].wait_recv()
+        attended = attended + rs[i, :, 0:QW].astype(F32)
+    attended = jnp.concatenate([attended, jnp.zeros((32, PW - QW), F32)], axis=1)
     att = attended.astype(BF)
     halves = jnp.concatenate([att[:, :HW], att[:, HW:]], axis=0)
     send[...] = (
@@ -182,7 +224,9 @@
     att_out[...] = att[:, :QW]
     weighted = (attended * gain[pl.ds(me_q, 1), :]).astype(BF)
     stats[...] = jnp.zeros(stats.shape, F32)
-    stats[:, 0:64] = jnp.dot(weighted[:, :QW], router[...], preferred_element_type=F32)
+    stats[:, 0:64] = lax.dot_general(
+        weighted[:, :QW], router[...], (((1,), (1,)), ((), ())), preferred_element_type=F32
+    )
     stats[:, 64:65] = jnp.sum(attended * attended, axis=1, keepdims=True)
 
     own_msg = pltpu.make_async_copy(send.at[0], recv.at[0, 0], a_rs.at[0])
@@ -206,23 +250,19 @@
     for copy in shared:
         copy.start()
 
-    loads[2].wait()
-    tail = jnp.zeros((4, 360, PW - QW), BF)
-    wda[:, :, QW:] = tail
-
-    def shift_rows(i, carry):
-        rows = pl.ds(pl.multiple_of(i * 16, 16), 16)
-        block = wd[rows, :].astype(F32)
+    for raw, out, load in ((wg, wga, loads[3]), (wu, wua, loads[4]), (wd, wda, loads[5])):
+        load.wait()
+        out[:, :, QW:] = jnp.zeros((4, 360, PW - QW), BF)
+
+        def shift_rows(i, carry, raw=raw, out=out):
+            rows = pl.ds(pl.multiple_of(i * 16, 16), 16)
+            for q in range(4):
+                out[q, rows, 0:QW] = raw[rows, QW * q : QW * (q + 1)]
+            return carry
+
+        lax.fori_loop(0, 22, shift_rows, 0)
         for q in range(4):
-            wda[q, rows, 0:QW] = block[:, QW * q : QW * (q + 1)].astype(BF)
-        return carry
-
-    lax.fori_loop(0, 22, shift_rows, 0)
-    block = wd[352:360, :].astype(F32)
-    for q in range(4):
-        wda[q, 352:360, 0:QW] = block[:, QW * q : QW * (q + 1)].astype(BF)
-    loads[0].wait()
-    loads[1].wait()
+            out[q, 352:360, 0:QW] = raw[352:360, QW * q : QW * (q + 1)]
 
     total = stats[...]
     for i, copy in enumerate(shared):
@@ -231,9 +271,9 @@
     scale = lax.rsqrt(total[:, 64:65] / (ND * QW) + EPS)
     logits = total[:, 0:64] * scale
     named = jnp.zeros((32, 64), jnp.bool_)
-    experts = lax.broadcasted_iota(jnp.int32, (32, 64), 1)
+    experts = lax.broadcasted_iota(jnp.int32, (32, 64), 1).astype(F32)
     for k in range(4):
-        named = named | (ids_col[0:32, k : k + 1] == experts)
+        named = named | (ids_col[k][0:32] == experts)
     lifted = jnp.where(named, jnp.exp(jnp.where(named, logits, 0.0)), 0.0)
     weight = lifted / jnp.sum(lifted, axis=1, keepdims=True)
     weight = jnp.concatenate([weight, weight], axis=0)
@@ -280,8 +320,8 @@
     def expert_out(b, forwards):
         for copy in forwards:
             copy.wait_recv()
-        gate = jnp.zeros((BR, wg.shape[1]), F32)
-        up = jnp.zeros((BR, wu.shape[1]), F32)
+        gate = jnp.zeros((BR, 360), F32)
+        up = jnp.zeros((BR, 360), F32)
         square = jnp.zeros((BR, 1), F32)
         for i, q in enumerate(blocks):
             rows = recv[i, span(b)].astype(F32).reshape(BM // 2, 2, 8, HW)
@@ -291,9 +331,9 @@
             feats = jnp.concatenate([low, high], axis=1)
             square = square + jnp.sum(feats * feats, axis=1, keepdims=True)
             feats = (feats * gain[pl.ds(q, 1), :]).astype(BF)
-            depth = pl.ds(pl.multiple_of(q * QW, 16), PW)
-            gate = gate + jnp.dot(feats, wg[depth, :], preferred_element_type=F32)
-            up = up + jnp.dot(feats, wu[depth, :], preferred_element_type=F32)
+            last = (((1,), (1,)), ((), ()))
+            gate = gate + lax.dot_general(feats, wga[q], last, preferred_element_type=F32)
+            up = up + lax.dot_general(feats, wua[q], last, preferred_element_type=F32)
         rms = lax.rsqrt(square / (ND * QW) + EPS)
         gate = gate * rms
         up = up * rms
@@ -402,33 +442,35 @@
     q_new, k_new, v_new, k_cache, v_cache, cache_len, cycle_start, residual, out_proj,
     norm_gain, router, route_ids, w_gate, w_up, w_down,
 ):
-    heads_out = attend(q_new, k_new, v_new, k_cache, v_cache, cache_len, cycle_start)
-    projected = jnp.dot(heads_out, out_proj, preferred_element_type=F32).astype(BF)
-    spare = PW - QW
-    proj = jnp.pad(
-        jnp.moveaxis(projected.reshape(-1, ND, QW), 1, 0), ((0, 0), (0, 0), (0, spare))
-    )
-    resid = jnp.pad(residual, ((0, 0), (0, spare)))
-    gain = jnp.pad(norm_gain.reshape(ND, QW), ((0, 0), (0, spare)))
-    ids_col = jnp.concatenate([route_ids, route_ids], axis=0)
-    ids_row = ids_col.T
     vmem = pl.BlockSpec(memory_space=pltpu.VMEM)
     hbm = pl.BlockSpec(memory_space=pl.ANY)
     dma = pltpu.SemaphoreType.DMA
-    half_ff = w_gate.shape[2]
+    ff = w_gate.shape[2]
+    tokens, heads = q_new.shape
+    wide = pltpu.VMEM((ff, ND * QW), BF)
+    cut = pltpu.VMEM((ND, ff, PW), BF)
     return pl.pallas_call(
         stage,
         out_shape=(
             jax.ShapeDtypeStruct(residual.shape, BF),
             jax.ShapeDtypeStruct(residual.shape, BF),
         ),
-        in_specs=[vmem] * 6 + [hbm] * 3,
+        in_specs=[vmem] * 3 + [hbm] * 2 + [vmem] * 3 + [hbm] + [vmem] * 3 + [hbm] * 3,
         out_specs=(vmem, vmem),
         scratch_shapes=[
-            pltpu.VMEM((ND * QW + 48, half_ff), BF),
-            pltpu.VMEM((ND * QW + 48, half_ff), BF),
-            pltpu.VMEM((half_ff, ND * QW), BF),
-            pltpu.VMEM((ND, half_ff, PW), BF),
+            pltpu.VMEM(k_cache.shape, BF),
+            pltpu.VMEM(v_cache.shape, BF),
+            pltpu.VMEM((tokens, heads // 128, 128), F32),
+            pltpu.VMEM((tokens, heads // 128, 128), F32),
+            pltpu.VMEM((ND * QW, heads), BF),
+            pltpu.VMEM((ND, tokens, PW), BF),
+            pltpu.VMEM((ND, PW), F32),
+            wide,
+            wide,
+            wide,
+            cut,
+            cut,
+            cut,
             pltpu.VMEM((3, 32, PW), BF),
             pltpu.VMEM((32, 128), F32),
             pltpu.VMEM((3, 32, 128), F32),
@@ -441,7 +483,7 @@
             pltpu.VMEM((NB, 3, BR, PW), F32),
             pltpu.VMEM((NG, 8, HW), BF),
             pltpu.VMEM((NG, 8, HW), BF),
-            dma((3,)),
+            dma((6,)),
             dma((3,)),
             dma((3,)),
             dma((3,)),
@@ -458,11 +500,13 @@
             dma((NB, 2)),
             dma,
             dma((NB,)),
-            dma,
         ],
         compiler_params=pltpu.CompilerParams(collective_id=0, has_side_effects=True),
         name="experts",
-    )(proj, resid, gain, router, ids_row, ids_col, w_gate[0], w_up[0], w_down[0])
+    )(
+        q_new, k_new, v_new, k_cache, v_cache, cache_len[None], cycle_start[None], residual,
+        out_proj.T, norm_gain[None], router.T, route_ids.T, w_gate[0].T, w_up[0].T, w_down[0],
+    )
 
 
 def solution(mesh):

time: 97.9 us -> 75.4 us (0.77)
  local copies, waits for them, and re-layouts: 21.4 us -> 4.16 us
  matrix products: 6.07 us -> 0 us
  Pallas kernels: 66.6 us -> 70.3 us
  other arithmetic: 2.43 us -> 0 us
    unnamed x11 -> x2, local copies, waits for them, and re-layouts: 13.7 us -> 2.84 us
    dot_general x4 -> x0, matrix products: 6.07 us -> none  [the longest x1 4.66 us: local(): jnp.dot(heads_out, out_proj, preferred_element_type=F32).astype(BF)]
    pallas_call x1, Pallas kernels: 66.6 us -> 70.3 us  [local(): pl.pallas_call(stage, out_shape=(jax.ShapeDtypeStruct(residual.shape, BF)...]
    reshape x5 -> x0, local copies, waits for them, and re-layouts: 2.87 us -> none  [the longest x1 0.99 us: attend(): queries = q_new.reshape(tokens, kv_local, grouped, HD)]
    pad x3 -> x0, local copies, waits for them, and re-layouts: 2.73 us -> none  [the longest x1 1.43 us: local(): resid = jnp.pad(residual, ((0, 0), (0, spare)))]
    concatenate x1 -> x0, other arithmetic: 1.38 us -> none  [local(): ids_col = jnp.concatenate([route_ids, route_ids], axis=0)]
    broadcast_in_dim x0 -> x1, local copies, waits for them, and re-layouts: none -> 1.32 us  [local(): norm_gain[None]]
    convert_element_type x3 -> x0, local copies, waits for them, and re-layouts: 1.01 us -> none  [the longest x1 0.78 us: attend(): own_value.astype(jnp.float32)[:, :, None, :]]
where the time goes in v2:
time: 75.4 us; the launch traced here: 75.1 us
  Pallas kernels  70.3 us (93%)
  local copies, waits for them, and re-layouts  4.16 us (6%)
    pallas_call x1, Pallas kernels, local(): pl.pallas_call(stage, out_shape=(jax.ShapeDtypeStruct(residual.shape, BF)...  70.3 us
    unnamed x2, local copies, waits for them, and re-layouts  2.84 us

profile of v2, /device:TPU:1, one launch (start us, length us, event | category | flops | bytes accessed | tf_op | source)
XLA Modules:
  0.0 75.1 jit_solution(3861947133515530938)
XLA Ops:
  0.6 1.3 %broadcast_in_dim.11.gain_row = f32[1,2880]{1,0:T(1,128)} reshape(f32[2880]{0:T(1024)} %param.24) | data formatting | bytes 23040 | tf_op jit(solution)/shard_map/broadcast_in_dim | solution.py:508
  1.9 70.3 %experts.1 = (bf16[32,720]{1,0:T(8,128)(2,1)}, bf16[32,720]{1,0:T(8,128)(2,1)}) custom-call(bf16[32,1024]{1,0:T(8,128)(2,1)} %q_ref.1, bf16[32,128]{1,0:T(8,128)(2,1)} %k_new.1, bf16[32,128]{1,0:T(8,128)(2,1)} %v_new.1, bf16[32,128,128]{2,1,0:T(8,128)(2,1)} %k_hbm.1, bf16[32,128,128]{2,1,0:T(8,128)(2,1)} %v_hbm.1, s32[1,32]{1,0:T(1,128)} %bitcast.18, ...), custom_call_target="tpu_custom_call" | custom-call | tf_op jit(solution)/shard_map/experts/pallas_call | solution.py:452
  72.3 1.4 %copy.19 = bf16[32,720]{1,0:T(8,128)(2,1)} copy(bf16[32,720]{1,0:T(8,128)(2,1)} %get-tuple-element.4) | data formatting | bytes 92160
  73.7 1.4 %copy.20 = bf16[32,720]{1,0:T(8,128)(2,1)} copy(bf16[32,720]{1,0:T(8,128)(2,1)} %get-tuple-element.5) | data formatting | bytes 92160

commit v3 on v2

--- a/solution.py
+++ b/solution.py
@@ -12,6 +12,8 @@
 PW = 768
 HW = PW // 2
 NG = 64
+NJ = 4
+JM = NG // NJ
 NB = 4
 BM = NG // NB
 BR = BM * 4
@@ -78,15 +80,16 @@
 
 
 def grp_shift(z, y, c, k, sign):
-    j = k // 8
-    half = (j + 1) // 2
-    dz = (j % 2) * half + (1 - j % 2) * (8 - half)
-    dy = (k // 2) % 4
-    dc = k % 2
+    j = lax.div(k, 8)
+    half = lax.div(j + 1, 2)
+    odd = lax.rem(j, 2)
+    dz = odd * half + (1 - odd) * (8 - half)
+    dy = lax.rem(lax.div(k, 2), 4)
+    dc = lax.rem(k, 2)
     if sign < 0:
         dz = 8 - dz
         dy = 4 - dy
-    return (((z + dz) % 8) * 4 + (y + dy) % 4) * 2 + (c + dc) % 2
+    return (lax.rem(z + dz, 8) * 4 + lax.rem(y + dy, 4)) * 2 + lax.rem(c + dc, 2)
 
 
 def wait_bytes(ref, sem):
@@ -118,16 +121,17 @@
     blocks = (me_q, left_q, right_q, opp_q)
 
     barrier = pltpu.get_barrier_semaphore()
+
+    def greet(k, carry):
+        pl.semaphore_signal(
+            barrier, inc=1, device_id={"grp": grp_shift(z, y, c, NG - k, 1)},
+            device_id_type=MESH,
+        )
+        return carry
+
+    lax.fori_loop(1, NG, greet, 0)
     for peer in peers:
         pl.semaphore_signal(barrier, inc=1, device_id=peer, device_id_type=MESH)
-
-    def greet(k, carry):
-        pl.semaphore_signal(
-            barrier, inc=1, device_id={"grp": grp_shift(z, y, c, k, 1)}, device_id_type=MESH
-        )
-        return carry
-
-    lax.fori_loop(1, NG, greet, 0)
     loads = [
         pltpu.make_async_copy(src, dst, w_sem.at[i])
         for i, (src, dst) in enumerate(
@@ -141,11 +145,11 @@
         load.start()
     gain[...] = jnp.zeros(gain.shape, F32)
     for q in range(4):
-        gain[q : q + 1, 0:QW] = gain_row[:, QW * q : QW * (q + 1)]
+        gain[q : q + 1, 0:QW] = gain_row[QW * q : QW * (q + 1)].reshape(1, QW)
         proj[q, :, QW:] = jnp.zeros((32, PW - QW), BF)
 
     def experts_of(rows):
-        return grp_shift(z, y, c, rows // 8, 1), (rows // 4) % 2, rows % 4
+        return grp_shift(z, y, c, lax.div(rows, 8), 1), lax.rem(lax.div(rows, 4), 2), lax.rem(rows, 4)
 
     slot = lax.broadcasted_iota(jnp.int32, (NG * 8, 1), 0)
     expert, part, rank = experts_of(slot)
@@ -195,7 +199,20 @@
     loads[1].wait()
     heads_out = attend(q_ref, k_new, v_new, keys, values, lens, starts, qs, hs)
     loads[2].wait()
-    pl.semaphore_wait(barrier, NG - 1 + 3)
+
+    def realign(raw, out, load):
+        load.wait()
+        out[:, :, QW:] = jnp.zeros((ND, 360, PW - QW), BF)
+
+        def shift_rows(i, carry):
+            rows = pl.ds(pl.multiple_of(i * 16, 16), 16)
+            for q in range(4):
+                out[q, rows, 0:QW] = raw[rows, QW * q : QW * (q + 1)]
+            return carry
+
+        lax.fori_loop(0, 22, shift_rows, 0)
+        for q in range(4):
+            out[q, 352:360, 0:QW] = raw[352:360, QW * q : QW * (q + 1)]
 
     sums = []
     for i, block in enumerate((opp_q, left_q, right_q, me_q)):
@@ -204,13 +221,14 @@
             heads_out, wo[rows, :], (((1,), (1,)), ((), ())), preferred_element_type=F32
         )
         proj[i, :, 0:QW] = part_sum.astype(BF)
-        if i < 3:
-            copy = pltpu.make_async_remote_copy(
-                src_ref=proj.at[i], dst_ref=rs.at[i], send_sem=rs_ss.at[i],
-                recv_sem=rs_rs.at[i], device_id=peers[i], device_id_type=MESH,
-            )
-            copy.start()
-            sums.append(copy)
+    pl.semaphore_wait(barrier, NG - 1 + 3)
+    for i in range(3):
+        copy = pltpu.make_async_remote_copy(
+            src_ref=proj.at[i], dst_ref=rs.at[i], send_sem=rs_ss.at[i],
+            recv_sem=rs_rs.at[i], device_id=peers[i], device_id_type=MESH,
+        )
+        copy.start()
+        sums.append(copy)
     attended = proj[3, :, 0:QW].astype(F32) + resid[...].astype(F32)
     for i in (1, 2, 0):
         sums[i].wait_recv()
@@ -221,6 +239,26 @@
     send[...] = (
         jnp.dot(pick, halves, preferred_element_type=F32).reshape(NG, 8, HW).astype(BF)
     )
+    own_msg = pltpu.make_async_copy(send.at[0], recv.at[0, 0], a_rs.at[0])
+    own_msg.start()
+
+    def post(j):
+        def post_one(k, carry):
+            pltpu.make_async_remote_copy(
+                src_ref=send.at[k], dst_ref=recv.at[0, k], send_sem=a_ss.at[j],
+                recv_sem=a_rs.at[j], device_id={"grp": grp_shift(z, y, c, k, 1)},
+                device_id_type=MESH,
+            ).start()
+            return carry
+
+        lax.fori_loop(max(1, j * JM), (j + 1) * JM, post_one, 0)
+
+    def posted(j):
+        first = max(1, j * JM)
+        wait_bytes(send.at[pl.ds(first, (j + 1) * JM - first)], a_ss.at[j])
+
+    for j in range(NJ):
+        post(j)
     att_out[...] = att[:, :QW]
     weighted = (attended * gain[pl.ds(me_q, 1), :]).astype(BF)
     stats[...] = jnp.zeros(stats.shape, F32)
@@ -229,17 +267,6 @@
     )
     stats[:, 64:65] = jnp.sum(attended * attended, axis=1, keepdims=True)
 
-    own_msg = pltpu.make_async_copy(send.at[0], recv.at[0, 0], a_rs.at[0])
-    own_msg.start()
-
-    def post(k, carry):
-        pltpu.make_async_remote_copy(
-            src_ref=send.at[k], dst_ref=recv.at[0, k], send_sem=a_ss, recv_sem=a_rs.at[k // BM],
-            device_id={"grp": grp_shift(z, y, c, k, 1)}, device_id_type=MESH,
-        ).start()
-        return carry
-
-    lax.fori_loop(1, NG, post, 0)
     shared = [
         pltpu.make_async_remote_copy(
             src_ref=stats, dst_ref=stats_in.at[i], send_sem=st_ss.at[i],
@@ -250,37 +277,9 @@
     for copy in shared:
         copy.start()
 
-    for raw, out, load in ((wg, wga, loads[3]), (wu, wua, loads[4]), (wd, wda, loads[5])):
-        load.wait()
-        out[:, :, QW:] = jnp.zeros((4, 360, PW - QW), BF)
-
-        def shift_rows(i, carry, raw=raw, out=out):
-            rows = pl.ds(pl.multiple_of(i * 16, 16), 16)
-            for q in range(4):
-                out[q, rows, 0:QW] = raw[rows, QW * q : QW * (q + 1)]
-            return carry
-
-        lax.fori_loop(0, 22, shift_rows, 0)
-        for q in range(4):
-            out[q, 352:360, 0:QW] = raw[352:360, QW * q : QW * (q + 1)]
-
-    total = stats[...]
-    for i, copy in enumerate(shared):
-        copy.wait_recv()
-        total = total + stats_in[i]
-    scale = lax.rsqrt(total[:, 64:65] / (ND * QW) + EPS)
-    logits = total[:, 0:64] * scale
-    named = jnp.zeros((32, 64), jnp.bool_)
-    experts = lax.broadcasted_iota(jnp.int32, (32, 64), 1).astype(F32)
-    for k in range(4):
-        named = named | (ids_col[k][0:32] == experts)
-    lifted = jnp.where(named, jnp.exp(jnp.where(named, logits, 0.0)), 0.0)
-    weight = lifted / jnp.sum(lifted, axis=1, keepdims=True)
-    weight = jnp.concatenate([weight, weight], axis=0)
-    w_high = weight.astype(BF)
-    w_low = (weight - w_high.astype(F32)).astype(BF)
-    mix_high = (jnp.dot(w_high, to_slot, preferred_element_type=F32) * pick_l).astype(BF)
-    mix_low = (jnp.dot(w_low, to_slot, preferred_element_type=F32) * pick_l).astype(BF)
+    realign(wg, wga, loads[3])
+    realign(wu, wua, loads[4])
+    realign(wd, wda, loads[5])
 
     first4 = lax.broadcasted_iota(jnp.int32, (BM // 2, 8, HW), 1) < 4
 
@@ -293,26 +292,27 @@
     def span(b):
         return pl.ds(b * BM, BM)
 
-    def ring_out(b):
-        wait_bytes(recv.at[0, span(b)], a_rs.at[b])
+    def ring_out(j):
+        at = pl.ds(j * JM, JM)
+        wait_bytes(recv.at[0, at], a_rs.at[j])
         copies = (
-            to_side(recv.at[0, span(b)], recv.at[1, span(b)], x_ss.at[b, 0], x_rs.at[b, 0], right),
-            to_side(recv.at[0, span(b)], recv.at[2, span(b)], x_ss.at[b, 1], x_rs.at[b, 1], left),
+            to_side(recv.at[0, at], recv.at[1, at], x_ss.at[j, 0], x_rs.at[j, 0], right),
+            to_side(recv.at[0, at], recv.at[2, at], x_ss.at[j, 1], x_rs.at[j, 1], left),
         )
         for copy in copies:
             copy.start()
         return copies
 
-    def ring_on(b, copies):
-        first, second = pl.ds(b * BM, BM // 2), pl.ds(b * BM + BM // 2, BM // 2)
+    def ring_on(j, copies):
+        first, second = pl.ds(j * JM, JM // 2), pl.ds(j * JM + JM // 2, JM // 2)
         copies[0].wait_recv()
         on_right = to_side(
-            recv.at[1, first], recv.at[3, first], f_ss.at[b, 0], f_rs.at[b, 0], right
+            recv.at[1, first], recv.at[3, first], f_ss.at[j, 0], f_rs.at[j, 0], right
         )
         on_right.start()
         copies[1].wait_recv()
         on_left = to_side(
-            recv.at[2, second], recv.at[3, second], f_ss.at[b, 1], f_rs.at[b, 1], left
+            recv.at[2, second], recv.at[3, second], f_ss.at[j, 1], f_rs.at[j, 1], left
         )
         on_left.start()
         return on_right, on_left
@@ -392,30 +392,46 @@
 
         lax.fori_loop(max(1, b * BM), (b + 1) * BM, post_back, 0)
 
-    out_c = [None] * NB
-    on_c = [None] * NB
+    out_c = [None] * NJ
+    on_c = [None] * NJ
     one_c = [None] * NB
     two_c = [None] * NB
-    out_c[0] = ring_out(0)
-    out_c[1] = ring_out(1)
-    on_c[0] = ring_on(0, out_c[0])
-    out_c[2] = ring_out(2)
-    on_c[1] = ring_on(1, out_c[1])
-    out_c[3] = ring_out(3)
-    one_c[0] = expert_out(0, on_c[0])
-    on_c[2] = ring_on(2, out_c[2])
-    one_c[1] = expert_out(1, on_c[1])
-    on_c[3] = ring_on(3, out_c[3])
-    two_c[0] = sum_on(0, one_c[0])
-    one_c[2] = expert_out(2, on_c[2])
-    two_c[1] = sum_on(1, one_c[1])
-    give_back(0, two_c[0])
-    one_c[3] = expert_out(3, on_c[3])
-    two_c[2] = sum_on(2, one_c[2])
-    give_back(1, two_c[1])
-    two_c[3] = sum_on(3, one_c[3])
-    give_back(2, two_c[2])
-    give_back(3, two_c[3])
+
+    def run(order):
+        for name, i in order:
+            if name == "o":
+                out_c[i] = ring_out(i)
+            elif name == "f":
+                on_c[i] = ring_on(i, out_c[i])
+            elif name == "e":
+                per = NJ // NB
+                forwards = [c for pair in on_c[i * per : (i + 1) * per] for c in pair]
+                one_c[i] = expert_out(i, forwards)
+            elif name == "s":
+                two_c[i] = sum_on(i, one_c[i])
+            else:
+                give_back(i, two_c[i])
+
+    plan = "o0o1f0o2f1o3e0f2e1f3s0e2s1g0e3s2g1s3g2g3"
+    run([(plan[n], int(plan[n + 1])) for n in range(0, len(plan), 2)])
+
+    total = stats[...]
+    for i, copy in enumerate(shared):
+        copy.wait_recv()
+        total = total + stats_in[i]
+    scale = lax.rsqrt(total[:, 64:65] / (ND * QW) + EPS)
+    logits = total[:, 0:64] * scale
+    named = jnp.zeros((32, 64), jnp.bool_)
+    experts = lax.broadcasted_iota(jnp.int32, (32, 64), 1).astype(F32)
+    for k in range(4):
+        named = named | (ids_col[k][0:32] == experts)
+    lifted = jnp.where(named, jnp.exp(jnp.where(named, logits, 0.0)), 0.0)
+    weight = lifted / jnp.sum(lifted, axis=1, keepdims=True)
+    weight = jnp.concatenate([weight, weight], axis=0)
+    w_high = weight.astype(BF)
+    w_low = (weight - w_high.astype(F32)).astype(BF)
+    mix_high = (jnp.dot(w_high, to_slot, preferred_element_type=F32) * pick_l).astype(BF)
+    mix_low = (jnp.dot(w_low, to_slot, preferred_element_type=F32) * pick_l).astype(BF)
 
     mixed = jnp.zeros((64, HW), F32)
     for b in range(NB):
@@ -430,12 +446,18 @@
 
     for copy in sums + shared:
         copy.wait_send()
-    wait_bytes(send.at[pl.ds(1, NG - 1)], a_ss)
+    for j in range(NJ):
+        posted(j)
     wait_bytes(rsend.at[pl.ds(1, NG - 1)], b_ss)
     for group in (out_c, on_c, one_c, two_c):
         for pair in group:
             for copy in pair:
                 copy.wait_send()
+
+
+def hand_on(att, mix, att_out, mix_out):
+    att_out[...] = att[...]
+    mix_out[...] = mix[...]
 
 
 def local(
@@ -448,8 +470,7 @@
     ff = w_gate.shape[2]
     tokens, heads = q_new.shape
     wide = pltpu.VMEM((ff, ND * QW), BF)
-    cut = pltpu.VMEM((ND, ff, PW), BF)
-    return pl.pallas_call(
+    att, mix = pl.pallas_call(
         stage,
         out_shape=(
             jax.ShapeDtypeStruct(residual.shape, BF),
@@ -468,9 +489,9 @@
             wide,
             wide,
             wide,
-            cut,
-            cut,
-            cut,
+            pltpu.VMEM((ND, ff, PW), BF),
+            pltpu.VMEM((ND, ff, PW), BF),
+            pltpu.VMEM((ND, ff, PW), BF),
             pltpu.VMEM((3, 32, PW), BF),
             pltpu.VMEM((32, 128), F32),
             pltpu.VMEM((3, 32, 128), F32),
@@ -488,12 +509,12 @@
             dma((3,)),
             dma((3,)),
             dma((3,)),
-            dma,
-            dma((NB,)),
-            dma((NB, 2)),
-            dma((NB, 2)),
-            dma((NB, 2)),
-            dma((NB, 2)),
+            dma((NJ,)),
+            dma((NJ,)),
+            dma((NJ, 2)),
+            dma((NJ, 2)),
+            dma((NJ, 2)),
+            dma((NJ, 2)),
             dma((NB, 2)),
             dma((NB, 2)),
             dma((NB, 2)),
@@ -505,8 +526,18 @@
         name="experts",
     )(
         q_new, k_new, v_new, k_cache, v_cache, cache_len[None], cycle_start[None], residual,
-        out_proj.T, norm_gain[None], router.T, route_ids.T, w_gate[0].T, w_up[0].T, w_down[0],
-    )
+        out_proj.T, norm_gain, router.T, route_ids.T, w_gate[0].T, w_up[0].T, w_down[0],
+    )
+    return pl.pallas_call(
+        hand_on,
+        out_shape=(
+            jax.ShapeDtypeStruct(residual.shape, BF),
+            jax.ShapeDtypeStruct(residual.shape, BF),
+        ),
+        in_specs=[vmem, vmem],
+        out_specs=(vmem, vmem),
+        name="hand_on",
+    )(att, mix)
 
 
 def solution(mesh):

time: 75.4 us -> 71.5 us (0.948)
  local copies, waits for them, and re-layouts: 4.16 us -> 0 us
    unnamed x2 -> x0, local copies, waits for them, and re-layouts: 2.84 us -> none
    pallas_call x0 -> x1, Pallas kernels: none -> 1.46 us  [local(): pl.pallas_call(hand_on, out_shape=(jax.ShapeDtypeStruct(residual.shape, B...]
    broadcast_in_dim x1 -> x0, local copies, waits for them, and re-layouts: 1.32 us -> none  [local(): norm_gain[None]]
    pallas_call x1, Pallas kernels: 70.3 us -> 69.2 us  [local(): pl.pallas_call(stage, out_shape=(jax.ShapeDtypeStruct(residual.shape, BF)...]
where the time goes in v3:
time: 71.5 us; the launch traced here: 71.3 us
  Pallas kernels  70.7 us (99%)
    pallas_call x1, Pallas kernels, local(): pl.pallas_call(stage, out_shape=(jax.ShapeDtypeStruct(residual.shape, BF)...  69.2 us
    pallas_call x1, Pallas kernels, local(): pl.pallas_call(hand_on, out_shape=(jax.ShapeDtypeStruct(residual.shape, B...  1.46 us

profile of v3, /device:TPU:1, one launch (start us, length us, event | category | flops | bytes accessed | tf_op | source)
XLA Modules:
  0.0 71.3 jit_solution(13494817789418467386)
XLA Ops:
  0.6 69.2 %experts.1 = (bf16[32,720]{1,0:T(8,128)(2,1)}, bf16[32,720]{1,0:T(8,128)(2,1)}) custom-call(bf16[32,1024]{1,0:T(8,128)(2,1)} %q_ref.1, bf16[32,128]{1,0:T(8,128)(2,1)} %k_new.1, bf16[32,128]{1,0:T(8,128)(2,1)} %v_new.1, bf16[32,128,128]{2,1,0:T(8,128)(2,1)} %k_hbm.1, bf16[32,128,128]{2,1,0:T(8,128)(2,1)} %v_hbm.1, s32[1,32]{1,0:T(1,128)} %bitcast.18, ...), custom_call_target="tpu_custom_call" | custom-call | tf_op jit(solution)/shard_map/experts/pallas_call | solution.py:473
  69.8 1.5 %hand_on.1 = (bf16[32,720]{1,0:T(8,128)(2,1)}, bf16[32,720]{1,0:T(8,128)(2,1)}) custom-call(bf16[32,720]{1,0:T(8,128)(2,1)} %get-tuple-element.4.att, bf16[32,720]{1,0:T(8,128)(2,1)} %get-tuple-element.5.mix), custom_call_target="tpu_custom_call" | custom-call | tf_op jit(solution)/shard_map/hand_on/pallas_call | solution.py:531

commit v4 on v3

--- a/solution.py
+++ b/solution.py
@@ -412,7 +412,7 @@
             else:
                 give_back(i, two_c[i])
 
-    plan = "o0o1f0o2f1o3e0f2e1f3s0e2s1g0e3s2g1s3g2g3"
+    plan = "o1o3f1o2f3o0e1f2e3f0s1e2s3g1e0s2g3s0g2g0"
     run([(plan[n], int(plan[n + 1])) for n in range(0, len(plan), 2)])
 
     total = stats[...]

time: 71.5 us -> 69.1 us (0.966)
  Pallas kernels: 70.7 us -> 68.3 us
    pallas_call x1, Pallas kernels: 69.2 us -> 66.8 us  [local(): pl.pallas_call(stage, out_shape=(jax.ShapeDtypeStruct(residual.shape, BF)...]
where the time goes in v4:
time: 69.1 us; the launch traced here: 68.9 us
  Pallas kernels  68.3 us (99%)
    pallas_call x1, Pallas kernels, local(): pl.pallas_call(stage, out_shape=(jax.ShapeDtypeStruct(residual.shape, BF)...  66.8 us
    pallas_call x1, Pallas kernels, local(): pl.pallas_call(hand_on, out_shape=(jax.ShapeDtypeStruct(residual.shape, B...  1.46 us

profile of v4, /device:TPU:1, one launch (start us, length us, event | category | flops | bytes accessed | tf_op | source)
XLA Modules:
  0.0 68.9 jit_solution(1794937767000591479)
XLA Ops:
  0.6 66.8 %experts.1 = (bf16[32,720]{1,0:T(8,128)(2,1)}, bf16[32,720]{1,0:T(8,128)(2,1)}) custom-call(bf16[32,1024]{1,0:T(8,128)(2,1)} %q_ref.1, bf16[32,128]{1,0:T(8,128)(2,1)} %k_new.1, bf16[32,128]{1,0:T(8,128)(2,1)} %v_new.1, bf16[32,128,128]{2,1,0:T(8,128)(2,1)} %k_hbm.1, bf16[32,128,128]{2,1,0:T(8,128)(2,1)} %v_hbm.1, s32[1,32]{1,0:T(1,128)} %bitcast.18, ...), custom_call_target="tpu_custom_call" | custom-call | tf_op jit(solution)/shard_map/experts/pallas_call | solution.py:473
  67.5 1.5 %hand_on.1 = (bf16[32,720]{1,0:T(8,128)(2,1)}, bf16[32,720]{1,0:T(8,128)(2,1)}) custom-call(bf16[32,720]{1,0:T(8,128)(2,1)} %get-tuple-element.4.att, bf16[32,720]{1,0:T(8,128)(2,1)} %get-tuple-element.5.mix), custom_call_target="tpu_custom_call" | custom-call | tf_op jit(solution)/shard_map/hand_on/pallas_call | solution.py:531
